TPU v7x, 32 devices: a whole 2x2x4 slice. The times are simulated.
32 devices in a mesh: seq: 8 (over z, y), samp: 4 (over x, core).
Axes of the slice: x: 2, y: 2, z: 4, core: 2. Of those that a mesh axis runs over, the one named last changes fastest.
Arguments:
- atoms: bfloat16 [48, 4096, 128], P('samp', 'seq'), may hold values from -3 to 3
- gain: float32 [128], replicated, may hold values from 0.25 to 1.75
- w_query: bfloat16 [128, 128], replicated, may hold values from -0.5 to 0.5
- w_key: bfloat16 [128, 128], replicated, may hold values from -0.5 to 0.5
- w_value: bfloat16 [128, 128], replicated, may hold values from -0.5 to 0.5
- w_gate: bfloat16 [128, 128], replicated, may hold values from -0.5 to 0.5
- w_out: bfloat16 [128, 128], replicated, may hold values from -0.5 to 0.5
- w_token: bfloat16 [128, 768], replicated, may hold values from -0.5 to 0.5
- w_pair: bfloat16 [16, 4], replicated, may hold values from -1.5 to 1.5
- pair_cond: bfloat16 [128, 32, 2048], P('seq'), may hold values from -6 to 6
- counts: int32 [8], replicated, may hold values from 472 to 512, as said below
- membership: int32 [4096], P('seq'), may hold values from 0 to 383, as said below
- pooled_cot: bfloat16 [48, 384, 768], P('samp', 'seq'), may hold values from -6 to 6
Outputs:
- pooled: bfloat16 [48, 384, 768], P('samp', 'seq')
- grad_atoms: bfloat16 [48, 4096, 128], P('samp', 'seq')
- grad_gain: float32 [128], replicated
- grad_query: float32 [128, 128], replicated
- grad_key: float32 [128, 128], replicated
- grad_value: float32 [128, 128], replicated
- grad_gate: float32 [128, 128], replicated
- grad_out: float32 [128, 128], replicated
- grad_token: float32 [128, 768], replicated
- grad_pair: float32 [16, 4], replicated
Inputs may be any that keep to these rules, and one draw needn't show every extreme that they name: `counts`: live atoms fill the first slots of each shard; some shard is full. `membership`: slots of shard s name tokens s * 48 to (s + 1) * 48 - 1, never falling along the slots; every token has one or more live atoms; slots past the shard's count name its last token.
All inputs are finite; a program needn't handle non-finite values.
Results may differ from a plain program's by a relative error of at most 0.012.
Values may be sent and summed in bfloat16 or wider, within the bound.
A program may use at most 128 MiB of HBM per device.

v0:
```python
import jax
import jax.numpy as jnp
from jax import lax
from jax.sharding import PartitionSpec as P

HEADS = 4
QBLK = 32
KWIN = 128
TOK_DEV = 48


epsilon = 1e-05
highest = lax.Precision.HIGHEST


def with_halo(block, sides, width):
    for axis, dim in sides:
        count = lax.axis_size(axis)
        forward = [(i, i + 1) for i in range(count - 1)]
        backward = [(target, source) for source, target in forward]
        low = lax.ppermute(
            lax.slice_in_dim(block, block.shape[dim] - width, None, axis=dim), axis, forward
        )
        high = lax.ppermute(lax.slice_in_dim(block, 0, width, axis=dim), axis, backward)
        block = jnp.concatenate([low, block, high], axis=dim)
    return block


def shifted(block, axis, distance):
    devices = range(lax.axis_size(axis))
    route = [(i - distance, i) for i in devices if i - distance in devices]
    return lax.ppermute(block, axis, route)


def windows(extended, blocks):
    span_blocks = KWIN // QBLK
    blocked = extended.reshape((blocks + span_blocks - 1, QBLK) + extended.shape[1:])
    return jnp.concatenate(
        [blocked[offset : offset + blocks] for offset in range(span_blocks)], axis=1
    )


def unwindow(grad_windows, blocks):
    span_blocks = KWIN // QBLK
    summed = None
    for offset in range(span_blocks):
        grad_piece = grad_windows[:, offset * QBLK : (offset + 1) * QBLK]
        pad_widths = [(offset, span_blocks - 1 - offset)] + [(0, 0)] * (grad_piece.ndim - 1)
        padded = jnp.pad(grad_piece, pad_widths)
        summed = padded if summed is None else summed + padded
    return summed.reshape((QBLK * (blocks + span_blocks - 1),) + grad_windows.shape[2:])


def sample_pass(
    atoms,
    queries,
    keys_ext,
    values_ext,
    gate_pre,
    key_mask,
    pair_bias,
    w_out,
    w_token,
    member,
    inv_count,
    atom_inv,
    cotangent,
):
    atom_rows, model_width = atoms.shape
    blocks = atom_rows // QBLK
    head_dim = model_width // HEADS
    scaling = head_dim ** (-0.5)
    query_heads = queries.reshape(blocks, QBLK, HEADS, head_dim)
    key_heads = windows(keys_ext, blocks).reshape(blocks, KWIN, HEADS, head_dim)
    value_heads = windows(values_ext, blocks).reshape(blocks, KWIN, HEADS, head_dim)
    scores = (
        jnp.einsum("bihd,bjhd->bhij", query_heads, key_heads, preferred_element_type=jnp.float32)
        * scaling
        + pair_bias
    )
    exp_scores = jnp.where(key_mask[:, None, None, :], jnp.exp(scores), 0.0)
    attn_probs = exp_scores / jnp.sum(exp_scores, axis=-1, keepdims=True)
    probs_low = attn_probs.astype(jnp.bfloat16)
    attended = jnp.einsum(
        "bhij,bjhd->bihd", probs_low, value_heads, preferred_element_type=jnp.float32
    ).reshape(atom_rows, model_width)
    gate_sig = jax.nn.sigmoid(gate_pre)
    gated_out = (gate_sig * attended).astype(jnp.bfloat16)
    updated = (
        atoms.astype(jnp.float32) + jnp.dot(gated_out, w_out, preferred_element_type=jnp.float32)
    ).astype(jnp.bfloat16)
    token_pre = jnp.dot(updated, w_token, preferred_element_type=jnp.float32)
    token_sig = jax.nn.sigmoid(token_pre)
    token_act = (token_pre * token_sig).astype(jnp.bfloat16)
    pooled = (
        jnp.einsum("at,ac->tc", member, token_act, preferred_element_type=jnp.float32)
        * inv_count[:, None]
    ).astype(jnp.bfloat16)
    grad_act = jnp.dot(member, cotangent, preferred_element_type=jnp.float32) * atom_inv[:, None]
    grad_pre = (grad_act * token_sig * (1.0 + token_pre * (1.0 - token_sig))).astype(jnp.bfloat16)
    grad_tokw = lax.dot_general(
        updated, grad_pre, (((0,), (0,)), ((), ())), preferred_element_type=jnp.float32
    )
    grad_updated = lax.dot_general(
        grad_pre, w_token, (((1,), (1,)), ((), ())), preferred_element_type=jnp.float32
    ).astype(jnp.bfloat16)
    grad_outw = lax.dot_general(
        gated_out, grad_updated, (((0,), (0,)), ((), ())), preferred_element_type=jnp.float32
    )
    grad_gated = lax.dot_general(
        grad_updated, w_out, (((1,), (1,)), ((), ())), preferred_element_type=jnp.float32
    )
    grad_gatepre = (grad_gated * attended * gate_sig * (1.0 - gate_sig)).astype(jnp.bfloat16)
    grad_att = (grad_gated * gate_sig).astype(jnp.bfloat16)
    grad_heads = grad_att.reshape(blocks, QBLK, HEADS, head_dim)
    grad_probs = jnp.einsum(
        "bihd,bjhd->bhij", grad_heads, value_heads, preferred_element_type=jnp.float32
    )
    grad_scores = attn_probs * (
        grad_probs - jnp.sum(attn_probs * grad_probs, axis=-1, keepdims=True)
    )
    scores_low = grad_scores.astype(jnp.bfloat16)
    grad_queries = (
        jnp.einsum(
            "bhij,bjhd->bihd", scores_low, key_heads, preferred_element_type=jnp.float32
        ).reshape(atom_rows, model_width)
        * scaling
    )
    grad_key_win = (
        jnp.einsum(
            "bhij,bihd->bjhd", scores_low, query_heads, preferred_element_type=jnp.float32
        ).reshape(blocks, KWIN, model_width)
        * scaling
    )
    grad_value_win = jnp.einsum(
        "bhij,bihd->bjhd", probs_low, grad_heads, preferred_element_type=jnp.float32
    ).reshape(blocks, KWIN, model_width)
    grad_kv_ext = jnp.stack([unwindow(grad_key_win, blocks), unwindow(grad_value_win, blocks)])
    return (
        pooled,
        grad_updated,
        grad_queries,
        grad_kv_ext,
        grad_gatepre,
        grad_outw,
        grad_tokw,
        grad_scores,
    )


def on_device(
    atoms,
    gain,
    w_query,
    w_key,
    w_value,
    w_gate,
    w_out,
    w_token,
    w_pair,
    pair_cond,
    counts,
    membership,
    pooled_cot,
):
    seq_count = lax.axis_size("seq")
    shard_pos = lax.axis_index("seq")
    samples, atom_rows, model_width = atoms.shape
    blocks = atom_rows // QBLK
    rim_width = (KWIN - QBLK) // 2
    slot_ids = jnp.arange(atom_rows, dtype=jnp.int32)
    rim_ids = jnp.arange(rim_width, dtype=jnp.int32)
    own_count = counts[shard_pos]
    left_count = counts[jnp.clip(shard_pos - 1, 0, seq_count - 1)]
    right_count = counts[jnp.clip(shard_pos + 1, 0, seq_count - 1)]
    alive_slots = slot_ids < own_count
    left_alive = (shard_pos > 0) & (atom_rows - rim_width + rim_ids < left_count)
    right_alive = (shard_pos < seq_count - 1) & (rim_ids < right_count)
    key_mask = windows(jnp.concatenate([left_alive, alive_slots, right_alive]), blocks)
    pair_f = pair_cond.reshape(blocks, QBLK, KWIN, pair_cond.shape[-1] // KWIN).astype(jnp.float32)
    pair_bias = jnp.einsum("bijc,ch->bhij", pair_f, w_pair.astype(jnp.float32))
    local_ids = membership - shard_pos * TOK_DEV
    member = (
        (local_ids[:, None] == jnp.arange(TOK_DEV, dtype=jnp.int32)[None, :]) & alive_slots[:, None]
    ).astype(jnp.bfloat16)
    member_f = member.astype(jnp.float32)
    inv_count = 1.0 / jnp.sum(member_f, axis=0)
    atom_inv = jnp.dot(member_f, inv_count, precision=highest)
    atoms_f = atoms.astype(jnp.float32)
    centred = atoms_f - jnp.mean(atoms_f, axis=-1, keepdims=True)
    variance = jnp.mean(centred * centred, axis=-1, keepdims=True)
    inv_std = lax.rsqrt(variance + epsilon)
    normed = centred * inv_std
    hidden = (normed * gain).astype(jnp.bfloat16)
    stacked_kv = jnp.stack([w_key, w_value])
    queries = jnp.einsum("san,nm->sam", hidden, w_query, preferred_element_type=jnp.float32).astype(
        jnp.bfloat16
    )
    gate_pre = jnp.einsum("san,nm->sam", hidden, w_gate, preferred_element_type=jnp.float32)
    kv_local = jnp.einsum(
        "san,knm->skam", hidden, stacked_kv, preferred_element_type=jnp.float32
    ).astype(jnp.bfloat16)
    kv_ext = with_halo(kv_local, (("seq", 2),), rim_width)

    def per_sample(totals, inputs):
        sample_atoms, sample_queries, sample_kv, sample_gate, cotangent = inputs
        (
            pooled,
            grad_updated,
            grad_queries,
            grad_kv_ext,
            grad_gatepre,
            grad_outw,
            grad_tokw,
            grad_scores,
        ) = sample_pass(
            sample_atoms,
            sample_queries,
            sample_kv[0],
            sample_kv[1],
            sample_gate,
            key_mask,
            pair_bias,
            w_out,
            w_token,
            member,
            inv_count,
            atom_inv,
            cotangent,
        )
        acc_out, acc_token, acc_scores = totals
        totals = (acc_out + grad_outw, acc_token + grad_tokw, acc_scores + grad_scores)
        return (totals, (pooled, grad_updated, grad_queries, grad_kv_ext, grad_gatepre))

    start = (
        jnp.zeros((model_width, model_width), jnp.float32),
        jnp.zeros((model_width, w_token.shape[1]), jnp.float32),
        jnp.zeros((blocks, HEADS, QBLK, KWIN), jnp.float32),
    )
    totals, outputs = lax.scan(per_sample, start, (atoms, queries, kv_ext, gate_pre, pooled_cot))
    acc_out, acc_token, score_sum = totals
    pooled, grad_updated, grad_queries, grad_kv_ext, grad_gatepre = outputs
    from_left = shifted(
        grad_kv_ext[:, :, atom_rows + rim_width :].astype(jnp.bfloat16), "seq", 1
    ).astype(jnp.float32)
    from_right = shifted(grad_kv_ext[:, :, :rim_width].astype(jnp.bfloat16), "seq", -1).astype(
        jnp.float32
    )
    inner = grad_kv_ext[:, :, rim_width : rim_width + atom_rows]
    grad_kv = jnp.concatenate(
        [
            inner[:, :, :rim_width] + from_left,
            inner[:, :, rim_width : atom_rows - rim_width],
            inner[:, :, atom_rows - rim_width :] + from_right,
        ],
        axis=2,
    ).astype(jnp.bfloat16)
    grad_q_low = grad_queries.astype(jnp.bfloat16)
    grad_qw = jnp.einsum("san,sam->nm", hidden, grad_q_low, preferred_element_type=jnp.float32)
    grad_kvw = jnp.einsum("san,skam->knm", hidden, grad_kv, preferred_element_type=jnp.float32)
    grad_gw = jnp.einsum("san,sam->nm", hidden, grad_gatepre, preferred_element_type=jnp.float32)
    grad_hidden = (
        jnp.einsum("sam,nm->san", grad_q_low, w_query, preferred_element_type=jnp.float32)
        + jnp.einsum("skam,knm->san", grad_kv, stacked_kv, preferred_element_type=jnp.float32)
        + jnp.einsum("sam,nm->san", grad_gatepre, w_gate, preferred_element_type=jnp.float32)
    )
    grad_gain_part = jnp.sum(grad_hidden * normed, axis=(0, 1))
    grad_normed = grad_hidden * gain
    grad_ln = inv_std * (
        grad_normed
        - jnp.mean(grad_normed, axis=-1, keepdims=True)
        - normed * jnp.mean(grad_normed * normed, axis=-1, keepdims=True)
    )
    grad_atoms = (grad_updated.astype(jnp.float32) + grad_ln).astype(jnp.bfloat16)
    grad_pair_part = jnp.einsum("bijc,bhij->ch", pair_f, score_sum)
    grad_gain, grad_query, grad_key, grad_value, grad_gate, grad_out, grad_token, grad_pair = (
        lax.psum(
            (
                grad_gain_part,
                grad_qw,
                grad_kvw[0],
                grad_kvw[1],
                grad_gw,
                acc_out,
                acc_token,
                grad_pair_part,
            ),
            ("seq", "samp"),
        )
    )
    return (
        pooled,
        grad_atoms,
        grad_gain,
        grad_query,
        grad_key,
        grad_value,
        grad_gate,
        grad_out,
        grad_token,
        grad_pair,
    )


def solution(mesh):
    placed = (
        P("samp", "seq", None),
        P(),
        P(),
        P(),
        P(),
        P(),
        P(),
        P(),
        P(),
        P("seq", None, None),
        P(),
        P("seq"),
        P("samp", "seq", None),
    )
    return jax.shard_map(
        on_device,
        mesh=mesh,
        in_specs=placed,
        out_specs=(
            P("samp", "seq", None),
            P("samp", "seq", None),
            P(),
            P(),
            P(),
            P(),
            P(),
            P(),
            P(),
            P(),
        ),
        check_vma=False,
    )
```

profile of v0, /device:TPU:0, one launch (start us, length us, event | category | flops | bytes accessed | tf_op | source)
XLA Modules:
  0.0 724.3 jit_solution(18286014864232860557)
XLA Ops:
  17.3 5.5 collective-permute-start
  27.4 2.4 fusion.76
  29.7 7.8 %copy.170 = bf16[16,32,2048]{1,2,0:T(8,128)(2,1)} copy(bf16[16,32,2048]{2,1,0:T(8,128)(2,1)} %param.24) | data formatting | bytes 4194304 | tf_op args[9]
  37.5 10.8 %copy.171 = bf16[16,32,128,16]{2,3,1,0:T(8,128)(2,1)} copy(bf16[16,32,128,16]{1,3,2,0:T(8,128)(2,1)} %bitcast.285) | data formatting | bytes 4194304 | tf_op jit(solution)/shard_map/reshape | solution.py:180
  54.2 5.2 pad_maximum_fusion.2
  59.5 484.6 %while.27 = (s32[]{:T(128)}, f32[128,128]{1,0:T(8,128)S(1)}, f32[128,768]{1,0:T(8,128)}, f32[16,4,32,128]{3,2,1,0:T(8,128)}, bf16[12,48,768]{2,1,0:T(8,128)(2,1)...) while((s32[]{:T(128)}, f32[128,128]{1,0:T(8,128)S(1)}, ...), condition=%wide.region_6.7_spmd.clone, body=%wide.region_3.6_spmd.clone.sunk | while | flops 545419648 | bytes 75287096 | solution.py:240
  88.2 2.3 multiply_reduce_fusion.3
  128.7 2.3 multiply_reduce_fusion.3
  169.0 2.3 multiply_reduce_fusion.3
  209.4 2.3 multiply_reduce_fusion.3
  249.7 2.3 multiply_reduce_fusion.3
  290.1 2.3 multiply_reduce_fusion.3
  330.5 2.3 multiply_reduce_fusion.3
  370.9 2.3 multiply_reduce_fusion.3
  411.2 2.3 multiply_reduce_fusion.3
  451.6 2.3 multiply_reduce_fusion.3
  492.0 2.3 multiply_reduce_fusion.3
  544.1 3.4 convolution_bitcast_fusion.2
  553.0 4.8 collective-permute-start.2
  560.5 9.4 %collective-permute-done.2 = bf16[12,2,48,128]{3,2,1,0:T(8,128)(2,1)S(1)} collective-permute-done((bf16[12,2,48,128]{3,2,1,0:T(8,128)(2,1)S(1)}, bf16[12,2,48,128]{3,2,1,0:T(8,128)(2,1)S(1)}, u32[]{:S(2)}, u32[]{:S(2)}) %collective-permute-start.2) | collective-permute-done | bytes 294944 | tf_op jit(solution)/shard_map/ppermute | solution.py:32
  571.7 3.0 fusion.51
  574.8 3.6 fusion.50
  579.9 41.4 %all-reduce.8 = (f32[128]{0:T(128)}, f32[16,4]{0,1:T(4,128)}) all-reduce(f32[128]{0:T(128)S(1)} %get-tuple-element.483, f32[16,4]{0,1:T(4,128)S(1)} %convolution_bitcast_fusion.4), channel_id=1, replica_groups=mesh['seq'=8,'samp'=4] {'seq','samp'}, use_global_device_ids=true, to_apply=%region_10.11 | all-reduce | flops 192 | bytes 1536 | tf_op jit(solution)/shard_map/psum | solution.py:277
  621.4 86.8 %all-reduce.12.cloned.1.call-done = (f32[128,128]{1,0:T(8,128)}, f32[128,128]{0,1:T(8,128)}, f32[128,128]{0,1:T(8,128)}, f32[128,128]{1,0:T(8,128)}, f32[128,128]{1,0:T(8,128)}, /*index=5*/f32[128,768]{1,0:T(8,128)}) async-done(((f32[128,128]{1,0:T(8,128)}, f32[128,128]{0,1:T(8,128)}, f32[128,128]{0,1:T(8,128)}, f32[128,128]{1,0:T(8,128)}, f32[128,128]{1,0:T(8,128)}, /*index=5*/f32[128,768]{1,0:T(8,128)}), ...) | async-done | bytes 720912 | tf_op jit(solution)/shard_map/psum | solution.py:277
  (1088 shorter events, 495.7 us)
Async XLA Ops:
  7.2 20.2 %copy-start = (bf16[128,128]{1,0:T(8,128)(2,1)S(1)}, bf16[128,128]{1,0:T(8,128)(2,1)}, u32[]{:S(2)}) copy-start(bf16[128,128]{1,0:T(8,128)(2,1)} %param.20) | copy-start | bytes 98308
  7.2 701.0 %all-reduce.12.cloned.1.call-start = ((), (), s32[]{:S(2)}) async-start(), calls=%async_computation | async-start | bytes 1441792 | tf_op jit(solution)/shard_map/psum | solution.py:277
  10.8 40.8 %copy-start.1 = (bf16[12,512,128]{1,2,0:T(8,128)(2,1)}, bf16[12,512,128]{1,2,0:T(8,128)(2,1)S(1)}, u32[]{:S(2)}) copy-start(bf16[12,512,128]{1,2,0:T(8,128)(2,1)S(1)} %copy.160) | copy-start | bytes 4718596
  11.0 40.5 %copy-start.20 = (f32[12,512]{1,0:T(8,128)}, f32[12,512]{1,0:T(8,128)S(1)}, u32[]{:S(2)}) copy-start(f32[12,512]{1,0:T(8,128)S(1)} %broadcast_multiply_fusion.2) | copy-start | bytes 73732
  11.5 40.0 %copy-start.23 = (f32[12,512]{1,0:T(8,128)}, f32[12,512]{1,0:T(8,128)S(1)}, u32[]{:S(2)}) copy-start(f32[12,512]{1,0:T(8,128)S(1)} %add_rsqrt_fusion) | copy-start | bytes 73732
  14.3 8.5 %copy-start.33 = (s32[8]{0:T(128)S(1)}, s32[8]{0:T(128)}, u32[]{:S(2)}) copy-start(s32[8]{0:T(128)} %param.25) | copy-start | bytes 100
  14.3 9.8 %copy-start.34 = (s32[512]{0:T(512)S(1)}, s32[512]{0:T(512)}, u32[]{:S(2)}) copy-start(s32[512]{0:T(512)} %param.26) | copy-start | bytes 6148
  15.7 38.1 %collective-permute-start.1 = (bf16[12,2,48,128]{3,2,1,0:T(8,128)(2,1)}, bf16[12,2,48,128]{3,2,1,0:T(8,128)(2,1)S(1)}, u32[]{:S(2)}, u32[]{:S(2)}) collective-permute-start(bf16[12,2,48,128]{3,2,1,0:T(8,128)(2,1)} %copy.166), channel_id=1, source_target_pairs={{4,0},{8,4},{12,8},{16,12},{20,16},{24,20},{28,24},{5,1},{9,5},{13... | collective-permute-start | bytes 884744 | tf_op jit(solution)/shard_map/ppermute | solution.py:24
  17.3 36.2 %collective-permute-start = (bf16[12,2,48,128]{3,2,1,0:T(8,128)(2,1)S(1)}, bf16[12,2,48,128]{3,2,1,0:T(8,128)(2,1)S(1)}, u32[]{:S(2)}, u32[]{:S(2)}) collective-permute-start(bf16[12,2,48,128]{3,2,1,0:T(8,128)(2,1)S(1)} %copy.165), channel_id=1, source_target_pairs={{0,4},{4,8},{8,12},{12,16},{16,20},{20,24},{24,28},{1,5},{5,9},{9,... | collective-permute-start | bytes 884744 | tf_op jit(solution)/shard_map/ppermute | solution.py:21
  37.5 10.8 %copy-start.35 = (bf16[16,4]{0,1:T(4,128)(2,1)S(1)}, bf16[16,4]{0,1:T(4,128)(2,1)}, u32[]{:S(2)}) copy-start(bf16[16,4]{0,1:T(4,128)(2,1)} %param.23) | copy-start | bytes 388
  59.5 484.6 %copy-start.21 = (f32[12,512]{1,0:T(8,128)S(1)}, f32[12,512]{1,0:T(8,128)}, u32[]{:S(2)}) copy-start(f32[12,512]{1,0:T(8,128)} %copy-done.20) | copy-start | bytes 73732
  59.5 484.6 %copy-start.32 = (f32[128]{0:T(128)S(1)}, f32[128]{0:T(128)}, u32[]{:S(2)}) copy-start(f32[128]{0:T(128)} %param.16) | copy-start | bytes 1540
  79.0 5.6 copy-start.4
  200.2 5.6 copy-start.4
  280.9 5.6 copy-start.4
  361.7 5.6 copy-start.4
  402.0 5.6 copy-start.4
  442.4 5.6 copy-start.4
  482.8 5.6 copy-start.4
  523.2 5.6 copy-start.4
  551.2 8.0 %copy-start.2 = (bf16[12,512,128]{1,2,0:T(8,128)(2,1)S(1)}, bf16[12,512,128]{1,2,0:T(8,128)(2,1)}, u32[]{:S(2)}) copy-start(bf16[12,512,128]{1,2,0:T(8,128)(2,1)} %copy-done.1) | copy-start | bytes 4718596
  551.2 8.0 %copy-start.24 = (f32[12,512]{1,0:T(8,128)S(1)}, f32[12,512]{1,0:T(8,128)}, u32[]{:S(2)}) copy-start(f32[12,512]{1,0:T(8,128)} %copy-done.23) | copy-start | bytes 73732
  553.0 16.8 %collective-permute-start.2 = (bf16[12,2,48,128]{3,2,1,0:T(8,128)(2,1)S(1)}, bf16[12,2,48,128]{3,2,1,0:T(8,128)(2,1)S(1)}, u32[]{:S(2)}, u32[]{:S(2)}) collective-permute-start(bf16[12,2,48,128]{3,2,1,0:T(8,128)(2,1)S(1)} %get-tuple-element.564), channel_id=1, source_target_pairs={{0,4},{4,8},{8,12},{12,16},{16,20},{20,24},{24,28},{1,5},{5,9},{9,... | collective-permute-start | bytes 884744 | tf_op jit(solution)/shard_map/ppermute | solution.py:32
  557.9 12.0 %collective-permute-start.3 = (bf16[12,2,48,128]{3,2,1,0:T(8,128)(2,1)S(1)}, bf16[12,2,48,128]{3,2,1,0:T(8,128)(2,1)S(1)}, u32[]{:S(2)}, u32[]{:S(2)}) collective-permute-start(bf16[12,2,48,128]{3,2,1,0:T(8,128)(2,1)S(1)} %get-tuple-element.565), channel_id=1, source_target_pairs={{4,0},{8,4},{12,8},{16,12},{20,16},{24,20},{28,24},{5,1},{9,5},{13... | collective-permute-start | bytes 884744 | tf_op jit(solution)/shard_map/ppermute | solution.py:32
  (162 other events, 362.3 us)
Sparse Core Ops, SparseCore 0:
  574.9 133.2 all-reduce.11
where the time goes:
time: 730 us; the launch traced here: 724 us
  local copies, waits for them, and re-layouts  222 us (30%)
  matrix products  212 us (29%)
  other arithmetic  120 us (16%)
  waiting for transfers between devices  96.2 us (13%)
  blocking collectives  41.4 us (6%)
  between operations  14.5 us (2%)
  starting transfers between devices  13 us (2%)
    psum x1, waiting for transfers between devices, on_device(): lax.psum((grad_gain_part, grad_qw, grad_kvw[0], grad_kvw[1], grad_gw, acc...  86.8 us
    psum x1, blocking collectives, on_device(): lax.psum((grad_gain_part, grad_qw, grad_kvw[0], grad_kvw[1], grad_gw, acc...  41.4 us
    concatenate x192, local copies, waits for them, and re-layouts, windows(): jnp.concatenate([blocked[offset:offset + blocks] for offset in range(span...  40.1 us
    dynamic_update_slice x24, other arithmetic, on_device(): lax.scan(per_sample, start, (atoms, queries, kv_ext, gate_pre, pooled_cot))  32.2 us
    unnamed x62, local copies, waits for them, and re-layouts  27.4 us
    div x12, other arithmetic, sample_pass(): attn_probs = exp_scores / jnp.sum(exp_scores, axis=-1, keepdims=True)  27.3 us
    dot_general x12, matrix products, sample_pass(): jnp.einsum('bhij,bihd->bjhd', probs_low, grad_heads, preferred_element_ty...  26.1 us
    dot_general x12, matrix products, sample_pass(): jnp.einsum('bhij,bjhd->bihd', probs_low, value_heads, preferred_element_t...  24.5 us
  transfers between devices with their start and end apart: 5, of which 2 were waited for; matrix products, arithmetic and copies ran while one was open for 5% of the time, Pallas kernels for 0%

commit v1 on v0

v1 whole, which is shorter than its diff:
```python
import functools

import jax
import jax.numpy as jnp
from jax import lax
from jax.experimental import pallas as pl
from jax.experimental.pallas import tpu as pltpu
from jax.sharding import PartitionSpec as P

HEADS = 4
QBLK = 32
KWIN = 128
LOG2E = 1.4426950408889634

epsilon = 1e-05
F32 = jnp.float32
BF16 = jnp.bfloat16
NN = (((1,), (0,)), ((), ()))
NT = (((1,), (1,)), ((), ()))
TN = (((0,), (0,)), ((), ()))
GROUP = 4
LANES = 128


def mm(a, b, dims=NN):
    return lax.dot_general(a, b, dims, preferred_element_type=F32)


def sigmoid(x):
    return 0.5 * jnp.tanh(0.5 * x) + 0.5


def layer_norm(x, gain):
    centred = x - jnp.mean(x, axis=-1, keepdims=True)
    variance = jnp.mean(centred * centred, axis=-1, keepdims=True)
    inv_std = lax.rsqrt(variance + epsilon)
    normed = centred * inv_std
    return normed, inv_std, (normed * gain).astype(BF16)


def head_lanes(width):
    lane = lax.broadcasted_iota(jnp.int32, (1, width), 1)
    return lane // (width // HEADS)


def expand(block, masks):
    return jnp.concatenate([block * m for m in masks], axis=0)


def collapse(wide, lane_head):
    rows = wide.shape[0] // HEADS
    out = wide[:rows]
    for h in range(1, HEADS):
        out = jnp.where(lane_head == h, wide[h * rows : (h + 1) * rows], out)
    return out


def lane_swap(parts, lane_block):
    count = len(parts)
    outs = []
    for b in range(count):
        out = None
        for a in range(count):
            shift = (QBLK * (a - b)) % LANES
            moved = parts[a] if shift == 0 else pltpu.roll(parts[a], shift, 1)
            out = moved if out is None else jnp.where(lane_block == a, moved, out)
        outs.append(out)
    return outs


def build_bias(counts_ref, pair_ref, wsm_ref, bias_scr, blocks, rows):
    pos = lax.axis_index("seq")
    size = lax.axis_size("seq")
    own = counts_ref[pos]
    left = jnp.where(pos > 0, counts_ref[jnp.maximum(pos - 1, 0)], 0)
    right = jnp.where(pos < size - 1, counts_ref[jnp.minimum(pos + 1, size - 1)], 0)
    rim = (KWIN - QBLK) // 2
    lane_block = head_lanes(LANES)
    chunk = wsm_ref.shape[1]
    per = wsm_ref.shape[0] // HEADS
    wsm = wsm_ref[...]
    for kk in range(pair_ref.shape[1] // chunk):
        biased = mm(wsm, pair_ref[:, kk * chunk : (kk + 1) * chunk], NT)
        for g in range(blocks // GROUP):
            parts = [
                biased[h * per : (h + 1) * per, g * LANES : (g + 1) * LANES] for h in range(HEADS)
            ]
            for w, out in enumerate(lane_swap(parts, lane_block)):
                b = g * GROUP + w
                slot = (
                    lax.broadcasted_iota(jnp.int32, (per, LANES), 0) + kk * per + b * QBLK - rim
                )
                alive = (
                    ((slot < 0) & (slot + rows < left))
                    | ((slot >= 0) & (slot < own))
                    | ((slot >= rows) & (slot - rows < right))
                )
                bias_scr[b, kk * per : (kk + 1) * per, :] = jnp.where(alive, out * LOG2E, -1e30)


def pair_gradient(pair_ref, score_scr, rsum_ref, blocks):
    lane_block = head_lanes(LANES)
    per = rsum_ref.shape[0] // HEADS
    chunk = rsum_ref.shape[1]
    total = None
    for kk in range(pair_ref.shape[1] // chunk):
        columns = []
        for g in range(blocks // GROUP):
            parts = [score_scr[g * GROUP + w, kk * per : (kk + 1) * per, :] for w in range(GROUP)]
            columns.append(jnp.concatenate(lane_swap(parts, lane_block), axis=0))
        grads = jnp.concatenate(columns, axis=1).astype(BF16)
        part = mm(grads, pair_ref[:, kk * chunk : (kk + 1) * chunk])
        total = part if total is None else total + part
    rsum_ref[...] = total


def main_kernel(
    counts_ref,
    atoms_ref,
    low_ref,
    high_ref,
    gain_ref,
    wq_ref,
    wk_ref,
    wv_ref,
    wg_ref,
    wo_ref,
    wt_ref,
    wsm_ref,
    pair_ref,
    ids_ref,
    cot_ref,
    pooled_ref,
    gupd_ref,
    dq_ref,
    dkv_ref,
    edge_low_ref,
    edge_high_ref,
    dg_ref,
    gout_ref,
    gtok_ref,
    rsum_ref,
    bias_scr,
    score_scr,
    member_scr,
    member_t_scr,
    inv_scr,
    wqg_scr,
    wkv_scr,
    hid_scr,
    q_scr,
    gate_scr,
    kv_scr,
    p_scr,
    plow_scr,
    att_scr,
    gatt_scr,
    acc_scr,
):
    step = pl.program_id(0)
    rows, width = q_scr.shape
    blocks = rows // QBLK
    rim = (KWIN - QBLK) // 2
    tokens = inv_scr.shape[0]
    scaling = (width // HEADS) ** (-0.5)
    lane_head = head_lanes(width)
    masks = [(lane_head == h).astype(F32).astype(BF16) for h in range(HEADS)]

    @pl.when(step == 0)
    def _():
        pos = lax.axis_index("seq")
        build_bias(counts_ref, pair_ref, wsm_ref, bias_scr, blocks, rows)
        token = lax.broadcasted_iota(jnp.int32, (tokens, rows), 0)
        slot = lax.broadcasted_iota(jnp.int32, (tokens, rows), 1)
        hit = (ids_ref[...] - pos * tokens == token) & (slot < counts_ref[pos])
        member_t = jnp.where(hit, 1.0, 0.0).astype(F32)
        inv_scr[...] = 1.0 / jnp.sum(member_t, axis=1, keepdims=True)
        member_t_scr[...] = member_t.astype(BF16)
        member_scr[...] = member_t.T.astype(BF16)
        wqg_scr[:, :width] = wq_ref[...]
        wqg_scr[:, width:] = wg_ref[...]
        wkv_scr[:, :width] = wk_ref[...]
        wkv_scr[:, width:] = wv_ref[...]
        score_scr[...] = jnp.zeros_like(score_scr)
        gout_ref[...] = jnp.zeros_like(gout_ref)
        gtok_ref[...] = jnp.zeros_like(gtok_ref)

    gain = gain_ref[...]
    x = atoms_ref[0].astype(F32)
    hid_scr[:rim] = layer_norm(low_ref[0].astype(F32), gain)[2]
    hid_scr[rim : rim + rows] = layer_norm(x, gain)[2]
    hid_scr[rim + rows :] = layer_norm(high_ref[0].astype(F32), gain)[2]
    kv_scr[...] = mm(hid_scr[...], wkv_scr[...]).astype(BF16)
    qg = mm(hid_scr[rim : rim + rows], wqg_scr[...])
    q_scr[...] = qg[:, :width].astype(BF16)
    gate_scr[...] = sigmoid(qg[:, width:])

    def forward(g, carry):
        for w in range(GROUP):
            b = g * GROUP + w
            at = pl.multiple_of(b * QBLK, QBLK)
            q_exp = expand(q_scr[pl.ds(at, QBLK), :], masks)
            keys = kv_scr[pl.ds(at, KWIN), :width]
            values = kv_scr[pl.ds(at, KWIN), width:]
            scores = mm(keys, q_exp, NT)
            e = jnp.exp2(scores * (scaling * LOG2E) + bias_scr[b])
            p = e * (1.0 / jnp.sum(e, axis=0, keepdims=True))
            p_scr[b] = p
            p_low = p.astype(BF16)
            plow_scr[b] = p_low
            att_scr[pl.ds(at, QBLK), :] = collapse(mm(p_low, values, TN), lane_head)
        return carry

    lax.fori_loop(0, blocks // GROUP, forward, 0)

    gate = gate_scr[...]
    att = att_scr[...]
    gated = (gate * att).astype(BF16)
    updated = (x + mm(gated, wo_ref[...])).astype(BF16)
    chunk = 256
    half = rows // 2
    scaled_cot = (cot_ref[0].astype(F32) * inv_scr[...]).astype(BF16)
    gupd = [None, None]
    for c in range(wt_ref.shape[1] // chunk):
        cols = slice(c * chunk, (c + 1) * chunk)
        wt = wt_ref[:, cols]
        pooled = None
        gtok = None
        for r in range(2):
            span = slice(r * half, (r + 1) * half)
            pre = mm(updated[span], wt)
            sig = sigmoid(pre)
            act = pre * sig
            grad_act = mm(member_scr[span, :], scaled_cot[:, cols])
            grad_pre = (grad_act * (sig + act * (1.0 - sig))).astype(BF16)
            part = mm(member_t_scr[:, span], act.astype(BF16))
            pooled = part if pooled is None else pooled + part
            part = mm(updated[span], grad_pre, TN)
            gtok = part if gtok is None else gtok + part
            part = mm(grad_pre, wt, NT)
            gupd[r] = part if gupd[r] is None else gupd[r] + part
        pooled_ref[0, :, cols] = (pooled * inv_scr[...]).astype(BF16)
        gtok_ref[:, cols] += gtok
    grad_updated = jnp.concatenate(gupd, axis=0).astype(BF16)
    gupd_ref[0] = grad_updated
    gout_ref[...] += mm(gated, grad_updated, TN)
    grad_gate = mm(grad_updated, wo_ref[...], NT) * gate
    gatt_scr[...] = grad_gate.astype(BF16)
    dg_ref[0] = (grad_gate * att * (1.0 - gate)).astype(BF16)
    acc_scr[...] = jnp.zeros_like(acc_scr)

    def backward(g, carry):
        for w in range(GROUP):
            b = g * GROUP + w
            at = pl.multiple_of(b * QBLK, QBLK)
            q_exp = expand(q_scr[pl.ds(at, QBLK), :], masks)
            g_exp = expand(gatt_scr[pl.ds(at, QBLK), :], masks)
            keys = kv_scr[pl.ds(at, KWIN), :width]
            values = kv_scr[pl.ds(at, KWIN), width:]
            p = p_scr[b]
            t = p * mm(values, g_exp, NT)
            ds = t - p * jnp.sum(t, axis=0, keepdims=True)
            score_scr[b] += ds
            ds_low = ds.astype(BF16)
            dq_ref[0, pl.ds(at, QBLK), :] = (
                collapse(mm(ds_low, keys, TN), lane_head) * scaling
            ).astype(BF16)
            acc_scr[pl.ds(at, KWIN), :width] += mm(ds_low, q_exp) * scaling
            acc_scr[pl.ds(at, KWIN), width:] += mm(plow_scr[b], g_exp)
        return carry

    lax.fori_loop(0, blocks // GROUP, backward, 0)
    edge_low_ref[0] = acc_scr[:rim].astype(BF16)
    edge_high_ref[0] = acc_scr[rim + rows :].astype(BF16)
    dkv_ref[0] = acc_scr[rim : rim + rows].astype(BF16)

    @pl.when(step == pl.num_programs(0) - 1)
    def _():
        pair_gradient(pair_ref, score_scr, rsum_ref, blocks)


def tail_kernel(
    atoms_ref,
    gain_ref,
    wq_ref,
    wk_ref,
    wv_ref,
    wg_ref,
    gupd_ref,
    dq_ref,
    dkv_ref,
    low_ref,
    high_ref,
    dg_ref,
    gatoms_ref,
    ggain_ref,
    gw_ref,
    d_scr,
    w_scr,
):
    step = pl.program_id(0)
    rows, width = atoms_ref.shape[1:]
    rim = low_ref.shape[1]

    @pl.when(step == 0)
    def _():
        for n, ref in enumerate((wq_ref, wk_ref, wv_ref, wg_ref)):
            w_scr[:, n * width : (n + 1) * width] = ref[...]
        ggain_ref[...] = jnp.zeros_like(ggain_ref)
        gw_ref[...] = jnp.zeros_like(gw_ref)

    gain = gain_ref[...]
    normed, inv_std, hidden = layer_norm(atoms_ref[0].astype(F32), gain)
    d_scr[:, :width] = dq_ref[0]
    d_scr[:, width : 3 * width] = dkv_ref[0]
    d_scr[:, 3 * width :] = dg_ref[0]
    d_scr[:rim, width : 3 * width] = (
        dkv_ref[0, :rim].astype(F32) + low_ref[0].astype(F32)
    ).astype(BF16)
    d_scr[rows - rim :, width : 3 * width] = (
        dkv_ref[0, rows - rim :].astype(F32) + high_ref[0].astype(F32)
    ).astype(BF16)
    d = d_scr[...]
    gw_ref[...] += mm(hidden, d, TN)
    grad_hidden = mm(d, w_scr[...], NT)
    gn = grad_hidden * normed
    ggain_ref[...] += jnp.sum(gn, axis=0, keepdims=True)
    gx = grad_hidden * gain
    grad_ln = inv_std * (
        gx
        - jnp.mean(gx, axis=-1, keepdims=True)
        - normed * jnp.mean(gn * gain, axis=-1, keepdims=True)
    )
    gatoms_ref[0] = (gupd_ref[0].astype(F32) + grad_ln).astype(BF16)


def per_sample(*shape):
    return pl.BlockSpec((1,) + shape, lambda s: (s,) + (0,) * len(shape))


def whole(*shape):
    return pl.BlockSpec(shape, lambda s: (0,) * len(shape))


def shifted(block, axis, distance):
    devices = range(lax.axis_size(axis))
    route = [(i - distance, i) for i in devices if i - distance in devices]
    return lax.ppermute(block, axis, route)


def on_device(
    atoms,
    gain,
    w_query,
    w_key,
    w_value,
    w_gate,
    w_out,
    w_token,
    w_pair,
    pair_cond,
    counts,
    membership,
    pooled_cot,
):
    samples, rows, width = atoms.shape
    blocks = rows // QBLK
    rim = (KWIN - QBLK) // 2
    tokens, token_width = pooled_cot.shape[1:]
    channels = w_pair.shape[0]
    per = 2 * LANES // channels
    low = shifted(atoms[:, rows - rim :], "seq", 1)
    high = shifted(atoms[:, :rim], "seq", -1)
    wsm = (
        w_pair.T[:, None, None, :] * jnp.eye(per, dtype=BF16)[None, :, :, None]
    ).reshape(HEADS * per, per * channels)
    pair2 = pair_cond.reshape(blocks * QBLK, pair_cond.shape[-1])
    gain2 = gain.reshape(1, width)
    square = whole(width, width)
    params = pltpu.CompilerParams(
        dimension_semantics=("arbitrary",), vmem_limit_bytes=56 * 1024 * 1024
    )
    shape = jax.ShapeDtypeStruct
    (pooled, gupd, dq, dkv, edge_low, edge_high, dg, gout, gtok, rsum) = pl.pallas_call(
        main_kernel,
        grid=(samples,),
        in_specs=[
            pl.BlockSpec(memory_space=pltpu.SMEM),
            per_sample(rows, width),
            per_sample(rim, width),
            per_sample(rim, width),
            whole(1, width),
            square,
            square,
            square,
            square,
            square,
            whole(width, token_width),
            whole(*wsm.shape),
            whole(*pair2.shape),
            whole(1, rows),
            per_sample(tokens, token_width),
        ],
        out_specs=[
            per_sample(tokens, token_width),
            per_sample(rows, width),
            per_sample(rows, width),
            per_sample(rows, 2 * width),
            per_sample(rim, 2 * width),
            per_sample(rim, 2 * width),
            per_sample(rows, width),
            square,
            whole(width, token_width),
            whole(*wsm.shape),
        ],
        out_shape=[
            shape((samples, tokens, token_width), BF16),
            shape((samples, rows, width), BF16),
            shape((samples, rows, width), BF16),
            shape((samples, rows, 2 * width), BF16),
            shape((samples, rim, 2 * width), BF16),
            shape((samples, rim, 2 * width), BF16),
            shape((samples, rows, width), BF16),
            shape((width, width), F32),
            shape((width, token_width), F32),
            shape(wsm.shape, F32),
        ],
        scratch_shapes=[
            pltpu.VMEM((blocks, KWIN, LANES), F32),
            pltpu.VMEM((blocks, KWIN, LANES), F32),
            pltpu.VMEM((rows, tokens), BF16),
            pltpu.VMEM((tokens, rows), BF16),
            pltpu.VMEM((tokens, 1), F32),
            pltpu.VMEM((width, 2 * width), BF16),
            pltpu.VMEM((width, 2 * width), BF16),
            pltpu.VMEM((rows + 2 * rim, width), BF16),
            pltpu.VMEM((rows, width), BF16),
            pltpu.VMEM((rows, width), F32),
            pltpu.VMEM((rows + 2 * rim, 2 * width), BF16),
            pltpu.VMEM((blocks, KWIN, LANES), F32),
            pltpu.VMEM((blocks, KWIN, LANES), BF16),
            pltpu.VMEM((rows, width), F32),
            pltpu.VMEM((rows, width), BF16),
            pltpu.VMEM((rows + 2 * rim, 2 * width), F32),
        ],
        compiler_params=params,
    )(
        counts,
        atoms,
        low,
        high,
        gain2,
        w_query,
        w_key,
        w_value,
        w_gate,
        w_out,
        w_token,
        wsm,
        pair2,
        membership.reshape(1, rows),
        pooled_cot,
    )
    from_left = shifted(edge_high, "seq", 1)
    from_right = shifted(edge_low, "seq", -1)
    grad_atoms, ggain, gw = pl.pallas_call(
        tail_kernel,
        grid=(samples,),
        in_specs=[
            per_sample(rows, width),
            whole(1, width),
            square,
            square,
            square,
            square,
            per_sample(rows, width),
            per_sample(rows, width),
            per_sample(rows, 2 * width),
            per_sample(rim, 2 * width),
            per_sample(rim, 2 * width),
            per_sample(rows, width),
        ],
        out_specs=[per_sample(rows, width), whole(1, width), whole(width, 4 * width)],
        out_shape=[
            shape((samples, rows, width), BF16),
            shape((1, width), F32),
            shape((width, 4 * width), F32),
        ],
        scratch_shapes=[
            pltpu.VMEM((rows, 4 * width), BF16),
            pltpu.VMEM((width, 4 * width), BF16),
        ],
        compiler_params=params,
    )(
        atoms,
        gain2,
        w_query,
        w_key,
        w_value,
        w_gate,
        gupd,
        dq,
        dkv,
        from_left,
        from_right,
        dg,
    )
    gpair = jnp.einsum("hjjc->ch", rsum.reshape(HEADS, per, per, channels))
    gout, gtok, gpair, ggain, gw = lax.psum((gout, gtok, gpair, ggain, gw), ("seq", "samp"))
    gq, gk, gv, gg = (gw[:, n * width : (n + 1) * width] for n in range(4))
    return (pooled, grad_atoms, ggain.reshape(width), gq, gk, gv, gg, gout, gtok, gpair)


def solution(mesh):
    placed = (
        P("samp", "seq", None),
        P(),
        P(),
        P(),
        P(),
        P(),
        P(),
        P(),
        P(),
        P("seq", None, None),
        P(),
        P("seq"),
        P("samp", "seq", None),
    )
    return jax.shard_map(
        on_device,
        mesh=mesh,
        in_specs=placed,
        out_specs=(
            P("samp", "seq", None),
            P("samp", "seq", None),
            P(),
            P(),
            P(),
            P(),
            P(),
            P(),
            P(),
            P(),
        ),
        check_vma=False,
    )
```

time: 730 us -> 343 us (0.47)
  local copies, waits for them, and re-layouts: 222 us -> 8.72 us
  matrix products: 212 us -> 0 us
  Pallas kernels: 0 us -> 159 us
  other arithmetic: 120 us -> 0.93 us
  waiting for transfers between devices: 96.2 us -> 105 us
    dot_general x180 -> x0, matrix products: 212 us -> none  [the longest x12 26.1 us: sample_pass(): jnp.einsum('bhij,bihd->bjhd', probs_low, grad_heads, preferred_element_ty...]
    pallas_call x0 -> x2, Pallas kernels: none -> 159 us  [the longest x1 146 us: on_device(): pl.pallas_call(main_kernel, grid=(samples,), in_specs=[pl.BlockSpec(memor...]
    reshape x73 -> x1, local copies, waits for them, and re-layouts: 43.6 us -> 0.19 us  [on_device(): gpair = jnp.einsum('hjjc->ch', rsum.reshape(HEADS, per, per, channels))]
    concatenate x192 -> x0, local copies, waits for them, and re-layouts: 40.1 us -> none  [windows(): jnp.concatenate([blocked[offset:offset + blocks] for offset in range(span...]
    dynamic_update_slice x24 -> x0, other arithmetic: 32.2 us -> none  [on_device(): lax.scan(per_sample, start, (atoms, queries, kv_ext, gate_pre, pooled_cot))]
    slice x46 -> x2, local copies, waits for them, and re-layouts: 34.8 us -> 2.65 us  [the longest x1 1.64 us: on_device(): gq, gk, gv, gg = (gw[:, n * width:(n + 1) * width] for n in range(4))]
    div x16 -> x0, other arithmetic: 27.8 us -> none  [the longest x12 27.3 us: sample_pass(): attn_probs = exp_scores / jnp.sum(exp_scores, axis=-1, keepdims=True)]
    convert_element_type x25 -> x1, other arithmetic: 25.2 us -> 0.01 us  [on_device(): jnp.eye(per, dtype=BF16)[None, :, :, None]]
  transfers between devices with their start and end apart: 5 -> 5, of which waited for: 2 -> 4; matrix products, arithmetic and copies ran while one was open for 5% -> 1% of each run, Pallas kernels for 0% -> 0%
where the time goes in v1:
time: 343 us; the launch traced here: 342 us
  Pallas kernels  159 us (46%)
  waiting for transfers between devices  105 us (31%)
  blocking collectives  42.1 us (12%)
  between operations  14.1 us (4%)
  starting transfers between devices  11.9 us (3%)
  local copies, waits for them, and re-layouts  8.72 us (3%)
    pallas_call x1, Pallas kernels, on_device(): pl.pallas_call(main_kernel, grid=(samples,), in_specs=[pl.BlockSpec(memor...  146 us
    psum x1, waiting for transfers between devices, on_device(): lax.psum((gout, gtok, gpair, ggain, gw), ('seq', 'samp'))  90.7 us
    psum x1, blocking collectives, on_device(): lax.psum((gout, gtok, gpair, ggain, gw), ('seq', 'samp'))  42.1 us
    ppermute x4, waiting for transfers between devices, shifted(): return lax.ppermute(block, axis, route)  14.7 us
    pallas_call x1, Pallas kernels, on_device(): pl.pallas_call(tail_kernel, grid=(samples,), in_specs=[per_sample(rows, w...  13.1 us
    ppermute x4, starting transfers between devices, shifted(): return lax.ppermute(block, axis, route)  11.8 us
  transfers between devices with their start and end apart: 5, of which 4 were waited for; matrix products, arithmetic and copies ran while one was open for 1% of the time, Pallas kernels for 0%

profile of v1, /device:TPU:0, one launch (start us, length us, event | category | flops | bytes accessed | tf_op | source)
XLA Modules:
  0.0 341.9 jit_solution(12247320222070664000)
XLA Ops:
  7.2 0.0 all-reduce.4.cloned.1.call-start
  7.2 1.0 fusion.1
  8.2 4.9 %collective-permute-start = (bf16[12,48,128]{2,1,0:T(8,128)(2,1)S(1)}, bf16[12,48,128]{2,1,0:T(8,128)(2,1)S(1)}, u32[]{:S(2)}, u32[]{:S(2)}) collective-permute-start(bf16[12,48,128]{2,1,0:T(8,128)(2,1)S(1)} %get-tuple-element.42), channel_id=1, source_target_pairs={{0,4},{4,8},{8,12},{12,16},{16,20},{20,24},{24,28},{1,5},{5,9},{9,... | collective-permute-start | bytes 442376 | tf_op jit(solution)/shard_map/ppermute | solution.py:348
  13.2 1.3 collective-permute-start.1
  14.5 0.8 broadcast_multiply_fusion
  15.3 0.9 mul.20.wsm_ref
  16.1 0.1 collective-permute-done.low_ref
  16.2 4.1 %collective-permute-done.1.high_ref = bf16[12,48,128]{2,1,0:T(8,128)(2,1)S(1)} collective-permute-done((bf16[12,48,128]{2,1,0:T(8,128)(2,1)S(1)}, bf16[12,48,128]{2,1,0:T(8,128)(2,1)S(1)}, u32[]{:S(2)}, u32[]{:S(2)}) %collective-permute-start.1) | collective-permute-done | bytes 147488 | tf_op jit(solution)/shard_map/ppermute | solution.py:348
  20.4 0.6 copy-done.3
  21.0 145.7 %shard_map.204 = (bf16[12,48,768]{2,1,0:T(8,128)(2,1)}, bf16[12,512,128]{2,1,0:T(8,128)(2,1)}, bf16[12,512,128]{2,1,0:T(8,128)(2,1)}, bf16[12,512,256]{2,1,0:T(8...) custom-call(s32[8]{0:T(128)} %counts_ref.1, ...), custom_call_target="tpu_custom_call" | custom-call | tf_op jit(solution)/shard_map/pallas_call | solution.py:384
  166.7 4.3 %collective-permute-start.2 = (bf16[12,48,256]{2,1,0:T(8,128)(2,1)}, bf16[12,48,256]{2,1,0:T(8,128)(2,1)S(1)}, u32[]{:S(2)}, u32[]{:S(2)}) collective-permute-start(bf16[12,48,256]{2,1,0:T(8,128)(2,1)} %get-tuple-element.27), channel_id=1, source_target_pairs={{0,4},{4,8},{8,12},{12,16},{16,20},{20,24},{24,28},{1,5},{5,9},{9,... | collective-permute-start | bytes 884744 | tf_op jit(solution)/shard_map/ppermute | solution.py:348
  171.0 1.3 collective-permute-start.3
  172.3 10.4 %collective-permute-done.2.low_ref = bf16[12,48,256]{2,1,0:T(8,128)(2,1)S(1)} collective-permute-done((bf16[12,48,256]{2,1,0:T(8,128)(2,1)}, bf16[12,48,256]{2,1,0:T(8,128)(2,1)S(1)}, u32[]{:S(2)}, u32[]{:S(2)}) %collective-permute-start.2) | collective-permute-done | bytes 294944 | tf_op jit(solution)/shard_map/ppermute | solution.py:348
  182.8 0.7 copy-done
  183.5 0.1 copy-done.1
  183.6 13.1 %shard_map.205 = (bf16[12,512,128]{2,1,0:T(8,128)(2,1)}, f32[1,128]{1,0:T(1,128)}, f32[128,512]{1,0:T(8,128)}) custom-call(bf16[12,512,128]{2,1,0:T(8,128)(2,1)} %atoms_ref.3, f32[1,128]{1,0:T(1,128)} %bitcast.12, bf16[128,128]{1,0:T(8,128)(2,1)} %wq_ref.3, bf16[128,128]{1,0:T(8,128)(2,1)} %wk_ref.3, bf16[128,128]{1,0:T(8,128)(2,1)} %wv_ref.3, ...), custom_call_target="tpu_custom_call" | custom-call | tf_op jit(solution)/shard_map/pallas_call | solution.py:466
  196.8 0.2 reshape.52
  197.0 0.1 select_reduce_fusion
  197.2 0.3 copy-done.5
  197.4 42.1 %all-reduce = (f32[128]{0:T(128)}, f32[16,4]{0,1:T(4,128)}) all-reduce(f32[128]{0:T(128)S(1)} %bitcast.14, f32[16,4]{0,1:T(4,128)S(1)} %bitcast.9), channel_id=1, replica_groups=mesh['seq'=8,'samp'=4] {'seq','samp'}, use_global_device_ids=true, to_apply=%region_0.0 | all-reduce | flops 192 | bytes 1536 | tf_op jit(solution)/shard_map/psum | solution.py:509
  239.5 90.7 %all-reduce.4.cloned.1.call-done = (f32[128,512]{1,0:T(8,128)}, f32[128,128]{1,0:T(8,128)}, f32[128,768]{1,0:T(8,128)}) async-done(((f32[128,512]{1,0:T(8,128)}, f32[128,128]{1,0:T(8,128)}, f32[128,768]{1,0:T(8,128)}), (f32[128,512]{1,0:T(8,128)}, f32[128,128]{1,0:T(8,128)}, f32[128,768]{1,0:T(8,128)})) %all-reduce.4.cloned.1.call-update) | async-done | bytes 720912 | tf_op jit(solution)/shard_map/psum | solution.py:509
  330.2 1.6 fusion.2
  331.8 1.5 copy.26
  333.3 1.8 copy.27
  (12 shorter events, 0.0 us)
Async XLA Ops:
  7.2 323.0 %all-reduce.4.cloned.1.call-start = ((), (), s32[]{:S(2)}) async-start(), calls=%async_computation | async-start | bytes 1441792 | tf_op jit(solution)/shard_map/psum | solution.py:509
  8.2 8.0 %collective-permute-start = (bf16[12,48,128]{2,1,0:T(8,128)(2,1)S(1)}, bf16[12,48,128]{2,1,0:T(8,128)(2,1)S(1)}, u32[]{:S(2)}, u32[]{:S(2)}) collective-permute-start(bf16[12,48,128]{2,1,0:T(8,128)(2,1)S(1)} %get-tuple-element.42), channel_id=1, source_target_pairs={{0,4},{4,8},{8,12},{12,16},{16,20},{20,24},{24,28},{1,5},{5,9},{9,... | collective-permute-start | bytes 442376 | tf_op jit(solution)/shard_map/ppermute | solution.py:348
  13.2 7.2 %collective-permute-start.1 = (bf16[12,48,128]{2,1,0:T(8,128)(2,1)S(1)}, bf16[12,48,128]{2,1,0:T(8,128)(2,1)S(1)}, u32[]{:S(2)}, u32[]{:S(2)}) collective-permute-start(bf16[12,48,128]{2,1,0:T(8,128)(2,1)S(1)} %get-tuple-element.41), channel_id=1, source_target_pairs={{4,0},{8,4},{12,8},{16,12},{20,16},{24,20},{28,24},{5,1},{9,5},{13... | collective-permute-start | bytes 442376 | tf_op jit(solution)/shard_map/ppermute | solution.py:348
  16.2 4.1 %copy-start.2 = (bf16[12,48,128]{2,1,0:T(8,128)(2,1)}, bf16[12,48,128]{2,1,0:T(8,128)(2,1)S(1)}, u32[]{:S(2)}) copy-start(bf16[12,48,128]{2,1,0:T(8,128)(2,1)S(1)} %collective-permute-done.low_ref) | copy-start | bytes 442372
  20.4 0.7 copy-start.3
  166.7 16.1 %collective-permute-start.2 = (bf16[12,48,256]{2,1,0:T(8,128)(2,1)}, bf16[12,48,256]{2,1,0:T(8,128)(2,1)S(1)}, u32[]{:S(2)}, u32[]{:S(2)}) collective-permute-start(bf16[12,48,256]{2,1,0:T(8,128)(2,1)} %get-tuple-element.27), channel_id=1, source_target_pairs={{0,4},{4,8},{8,12},{12,16},{16,20},{20,24},{24,28},{1,5},{5,9},{9,... | collective-permute-start | bytes 884744 | tf_op jit(solution)/shard_map/ppermute | solution.py:348
  171.0 11.7 %collective-permute-start.3 = (bf16[12,48,256]{2,1,0:T(8,128)(2,1)}, bf16[12,48,256]{2,1,0:T(8,128)(2,1)S(1)}, u32[]{:S(2)}, u32[]{:S(2)}) collective-permute-start(bf16[12,48,256]{2,1,0:T(8,128)(2,1)} %get-tuple-element.28), channel_id=1, source_target_pairs={{4,0},{8,4},{12,8},{16,12},{20,16},{24,20},{28,24},{5,1},{9,5},{13... | collective-permute-start | bytes 884744 | tf_op jit(solution)/shard_map/ppermute | solution.py:348
  182.8 0.7 copy-start
  182.8 0.9 copy-start.1
  183.6 13.2 %copy-start.4 = (f32[64,256]{1,0:T(8,128)S(1)}, f32[64,256]{1,0:T(8,128)}, u32[]{:S(2)}) copy-start(f32[64,256]{1,0:T(8,128)} %get-tuple-element.35) | copy-start | bytes 196612
  196.8 0.7 copy-start.5
Sparse Core Ops, SparseCore 0:
  196.9 133.1 all-reduce.3

commit v2 on v1

--- a/solution.py
+++ b/solution.py
@@ -195,23 +195,27 @@
     q_scr[...] = qg[:, :width].astype(BF16)
     gate_scr[...] = sigmoid(qg[:, width:])
 
-    def forward(g, carry):
-        for w in range(GROUP):
-            b = g * GROUP + w
-            at = pl.multiple_of(b * QBLK, QBLK)
-            q_exp = expand(q_scr[pl.ds(at, QBLK), :], masks)
-            keys = kv_scr[pl.ds(at, KWIN), :width]
-            values = kv_scr[pl.ds(at, KWIN), width:]
-            scores = mm(keys, q_exp, NT)
-            e = jnp.exp2(scores * (scaling * LOG2E) + bias_scr[b])
-            p = e * (1.0 / jnp.sum(e, axis=0, keepdims=True))
+    for g in range(blocks // GROUP):
+        spans = [g * GROUP + w for w in range(GROUP)]
+        q_exp = [expand(q_scr[b * QBLK : (b + 1) * QBLK, :], masks) for b in spans]
+        scores = [
+            mm(kv_scr[b * QBLK : b * QBLK + KWIN, :width], q, NT) for b, q in zip(spans, q_exp)
+        ]
+        es = [
+            jnp.exp2(sc * (scaling * LOG2E) + bias_scr[b]) for b, sc in zip(spans, scores)
+        ]
+        invs = [1.0 / jnp.sum(e, axis=0, keepdims=True) for e in es]
+        ps = [e * inv for e, inv in zip(es, invs)]
+        lows = [p.astype(BF16) for p in ps]
+        for b, p, low in zip(spans, ps, lows):
             p_scr[b] = p
-            p_low = p.astype(BF16)
-            plow_scr[b] = p_low
-            att_scr[pl.ds(at, QBLK), :] = collapse(mm(p_low, values, TN), lane_head)
-        return carry
-
-    lax.fori_loop(0, blocks // GROUP, forward, 0)
+            plow_scr[b] = low
+        wide = [
+            mm(low, kv_scr[b * QBLK : b * QBLK + KWIN, width:], TN)
+            for b, low in zip(spans, lows)
+        ]
+        for b, o in zip(spans, wide):
+            att_scr[b * QBLK : (b + 1) * QBLK, :] = collapse(o, lane_head)
 
     gate = gate_scr[...]
     att = att_scr[...]
@@ -247,29 +251,56 @@
     grad_gate = mm(grad_updated, wo_ref[...], NT) * gate
     gatt_scr[...] = grad_gate.astype(BF16)
     dg_ref[0] = (grad_gate * att * (1.0 - gate)).astype(BF16)
-    acc_scr[...] = jnp.zeros_like(acc_scr)
-
-    def backward(g, carry):
-        for w in range(GROUP):
-            b = g * GROUP + w
-            at = pl.multiple_of(b * QBLK, QBLK)
-            q_exp = expand(q_scr[pl.ds(at, QBLK), :], masks)
-            g_exp = expand(gatt_scr[pl.ds(at, QBLK), :], masks)
-            keys = kv_scr[pl.ds(at, KWIN), :width]
-            values = kv_scr[pl.ds(at, KWIN), width:]
-            p = p_scr[b]
-            t = p * mm(values, g_exp, NT)
-            ds = t - p * jnp.sum(t, axis=0, keepdims=True)
+
+    def tiles(x):
+        return [x[n * QBLK : (n + 1) * QBLK] for n in range(KWIN // QBLK)]
+
+    open_k = []
+    open_v = []
+
+    def close(first, count):
+        for n in range(count):
+            at = (first + n) * QBLK
+            acc_scr[at : at + QBLK, :width] = open_k[n] * scaling
+            acc_scr[at : at + QBLK, width:] = open_v[n]
+        del open_k[:count]
+        del open_v[:count]
+
+    def merge(opened, parts):
+        for n, part in enumerate(parts):
+            if n < len(opened):
+                opened[n] = opened[n] + part
+            else:
+                opened.append(part)
+
+    for g in range(blocks // GROUP):
+        spans = [g * GROUP + w for w in range(GROUP)]
+        g_exp = [expand(gatt_scr[b * QBLK : (b + 1) * QBLK, :], masks) for b in spans]
+        gps = [
+            mm(kv_scr[b * QBLK : b * QBLK + KWIN, width:], ge, NT) for b, ge in zip(spans, g_exp)
+        ]
+        dvs = [mm(plow_scr[b], ge) for b, ge in zip(spans, g_exp)]
+        ts = [p_scr[b] * gp for b, gp in zip(spans, gps)]
+        sums = [jnp.sum(t, axis=0, keepdims=True) for t in ts]
+        dss = [t - p_scr[b] * r for b, t, r in zip(spans, ts, sums)]
+        lows = [ds.astype(BF16) for ds in dss]
+        for b, ds in zip(spans, dss):
             score_scr[b] += ds
-            ds_low = ds.astype(BF16)
-            dq_ref[0, pl.ds(at, QBLK), :] = (
-                collapse(mm(ds_low, keys, TN), lane_head) * scaling
+        q_exp = [expand(q_scr[b * QBLK : (b + 1) * QBLK, :], masks) for b in spans]
+        dks = [mm(low, q) for low, q in zip(lows, q_exp)]
+        dqs = [
+            mm(low, kv_scr[b * QBLK : b * QBLK + KWIN, :width], TN)
+            for b, low in zip(spans, lows)
+        ]
+        for b, dk, dv in zip(spans, dks, dvs):
+            merge(open_k, tiles(dk))
+            merge(open_v, tiles(dv))
+            close(b, 1)
+        for b, dq in zip(spans, dqs):
+            dq_ref[0, b * QBLK : (b + 1) * QBLK, :] = (
+                collapse(dq, lane_head) * scaling
             ).astype(BF16)
-            acc_scr[pl.ds(at, KWIN), :width] += mm(ds_low, q_exp) * scaling
-            acc_scr[pl.ds(at, KWIN), width:] += mm(plow_scr[b], g_exp)
-        return carry
-
-    lax.fori_loop(0, blocks // GROUP, backward, 0)
+    close(blocks, len(open_k))
     edge_low_ref[0] = acc_scr[:rim].astype(BF16)
     edge_high_ref[0] = acc_scr[rim + rows :].astype(BF16)
     dkv_ref[0] = acc_scr[rim : rim + rows].astype(BF16)
@@ -332,6 +363,148 @@
         - normed * jnp.mean(gn * gain, axis=-1, keepdims=True)
     )
     gatoms_ref[0] = (gupd_ref[0].astype(F32) + grad_ln).astype(BF16)
+
+
+def axis_bits():
+    bits = []
+    for axis in ("samp", "seq"):
+        bit = 1
+        while bit < lax.axis_size(axis):
+            bits.append((axis, bit))
+            bit *= 2
+    return bits
+
+
+def sum_kernel(
+    gout_ref,
+    gtok_ref,
+    gw_ref,
+    rsum_ref,
+    ggain_ref,
+    gq_out,
+    gk_out,
+    gv_out,
+    gg_out,
+    gout_out,
+    gtok_out,
+    small_out,
+    buf,
+    gbuf,
+    send_sem,
+    recv_sem,
+    *slots,
+):
+    bits = axis_bits()
+    count = len(bits)
+    sends, recvs = slots[:count], slots[count:]
+    width = gout_ref.shape[0]
+    where = []
+    for axis, bit in bits:
+        me = lax.axis_index(axis)
+        upper = lax.rem(me // bit, 2)
+        where.append((upper, {axis: me + bit - 2 * bit * upper}))
+    barrier = pltpu.get_barrier_semaphore()
+    for _, partner in where:
+        pl.semaphore_signal(
+            barrier, inc=1, device_id=partner, device_id_type=pl.DeviceIdType.MESH
+        )
+
+    blocks = gtok_ref.shape[1] // width
+    for n in range(blocks):
+        buf[n * width : (n + 1) * width, :] = gtok_ref[:, n * width : (n + 1) * width]
+    for n in range(4):
+        at = (blocks + n) * width
+        buf[at : at + width, :] = gw_ref[:, n * width : (n + 1) * width]
+    at = (blocks + 4) * width
+    buf[at : at + width, :] = gout_ref[...]
+    at += width
+    buf[at:, :] = jnp.zeros((buf.shape[0] - at, width), F32)
+    high, wide = rsum_ref.shape
+    per = high // HEADS
+    row = lax.broadcasted_iota(jnp.int32, (high, wide), 0)
+    lane = lax.broadcasted_iota(jnp.int32, (high, wide), 1)
+    diagonal = jnp.where(lax.rem(row, per) == lane // (wide // per), rsum_ref[...], 0.0)
+    for h in range(HEADS):
+        line = jnp.sum(diagonal[h * per : (h + 1) * per], axis=0, keepdims=True)
+        for n in range(wide // width):
+            buf[at + n * HEADS + h : at + n * HEADS + h + 1, :] = line[
+                :, n * width : (n + 1) * width
+            ]
+    spot = at + HEADS * (wide // width)
+    buf[spot : spot + 1, :] = ggain_ref[...]
+    pl.semaphore_wait(barrier, count)
+
+    off = 0
+    length = buf.shape[0]
+    for k, (upper, partner) in enumerate(where):
+        length //= 2
+        keep = pl.multiple_of(off + upper * length, 16)
+        give = pl.multiple_of(off + (1 - upper) * length, 16)
+        sends[k][...] = buf[pl.ds(give, length), :].astype(BF16)
+        copy = pltpu.make_async_remote_copy(
+            src_ref=sends[k],
+            dst_ref=recvs[k],
+            send_sem=send_sem.at[k],
+            recv_sem=recv_sem.at[k],
+            device_id=partner,
+            device_id_type=pl.DeviceIdType.MESH,
+        )
+        copy.start()
+        copy.wait()
+        buf[pl.ds(keep, length), :] = buf[pl.ds(keep, length), :] + recvs[k][...].astype(F32)
+        off = keep
+    gbuf[pl.ds(off, length), :] = buf[pl.ds(off, length), :].astype(BF16)
+    for k in range(count - 1, -1, -1):
+        upper, partner = where[k]
+        part = gbuf.at[pl.ds(pl.multiple_of(off, 16), length), :]
+        copy = pltpu.make_async_remote_copy(
+            src_ref=part,
+            dst_ref=part,
+            send_sem=send_sem.at[count + k],
+            recv_sem=recv_sem.at[count + k],
+            device_id=partner,
+            device_id_type=pl.DeviceIdType.MESH,
+        )
+        copy.start()
+        copy.wait()
+        off = off - upper * length
+        length *= 2
+
+    def block(n):
+        return gbuf[n * width : (n + 1) * width, :].astype(F32)
+
+    for n in range(blocks):
+        gtok_out[:, n * width : (n + 1) * width] = block(n)
+    for n, ref in enumerate((gq_out, gk_out, gv_out, gg_out, gout_out)):
+        ref[...] = block(blocks + n)
+    small_out[...] = gbuf[at : at + small_out.shape[0], :].astype(F32)
+
+
+def sum_all(gout, gtok, gw, rsum, ggain):
+    shape = jax.ShapeDtypeStruct
+    width = gout.shape[0]
+    bits = axis_bits()
+    count = len(bits)
+    unit = 16 * 2**count
+    lines = gtok.shape[1] + gw.shape[1] + width + 16
+    total = -(-lines // unit) * unit
+    slots = [pltpu.VMEM((total >> (k + 1), width), BF16) for k in range(count)]
+    return pl.pallas_call(
+        sum_kernel,
+        in_specs=[pl.BlockSpec(memory_space=pltpu.VMEM)] * 5,
+        out_specs=[pl.BlockSpec(memory_space=pltpu.VMEM)] * 7,
+        out_shape=[shape((width, width), F32)] * 5
+        + [shape(gtok.shape, F32), shape((16, width), F32)],
+        scratch_shapes=[
+            pltpu.VMEM((total, width), F32),
+            pltpu.VMEM((total, width), BF16),
+            pltpu.SemaphoreType.DMA((2 * count,)),
+            pltpu.SemaphoreType.DMA((2 * count,)),
+        ]
+        + slots
+        + slots,
+        compiler_params=pltpu.CompilerParams(collective_id=0, has_side_effects=True),
+    )(gout, gtok, gw, rsum, ggain)
 
 
 def per_sample(*shape):
@@ -505,10 +678,12 @@
         from_right,
         dg,
     )
-    gpair = jnp.einsum("hjjc->ch", rsum.reshape(HEADS, per, per, channels))
-    gout, gtok, gpair, ggain, gw = lax.psum((gout, gtok, gpair, ggain, gw), ("seq", "samp"))
-    gq, gk, gv, gg = (gw[:, n * width : (n + 1) * width] for n in range(4))
-    return (pooled, grad_atoms, ggain.reshape(width), gq, gk, gv, gg, gout, gtok, gpair)
+    gq, gk, gv, gg, gout, gtok, small = sum_all(gout, gtok, gw, rsum, ggain)
+    halves = rsum.shape[1] // width
+    lines = small[: halves * HEADS].reshape(halves, HEADS, width // channels, channels)
+    gpair = jnp.sum(lines, axis=(0, 2)).T
+    ggain = small[halves * HEADS]
+    return (pooled, grad_atoms, ggain, gq, gk, gv, gg, gout, gtok, gpair)
 
 
 def solution(mesh):

time: 343 us -> 156 us (0.45)
  waiting for transfers between devices: 105 us -> 15.3 us
  Pallas kernels: 159 us -> 111 us
  blocking collectives: 42.1 us -> 0 us
  between operations: 14.1 us -> 0.72 us
  local copies, waits for them, and re-layouts: 8.72 us -> 14.5 us
    psum x1 -> x0, waiting for transfers between devices: 90.7 us -> none  [on_device(): lax.psum((gout, gtok, gpair, ggain, gw), ('seq', 'samp'))]
    pallas_call x1, Pallas kernels: 146 us -> 63.6 us  [on_device(): pl.pallas_call(main_kernel, grid=(samples,), in_specs=[pl.BlockSpec(memor...]
    psum x1 -> x0, blocking collectives: 42.1 us -> none  [on_device(): lax.psum((gout, gtok, gpair, ggain, gw), ('seq', 'samp'))]
    pallas_call x0 -> x1, Pallas kernels: none -> 33.9 us  [sum_all(): pl.pallas_call(sum_kernel, in_specs=[pl.BlockSpec(memory_space=pltpu.VMEM...]
    unnamed x14, local copies, waits for them, and re-layouts: 5.02 us -> 10.7 us
  transfers between devices with their start and end apart: 5 -> 4, of which waited for: 4 -> 3; matrix products, arithmetic and copies ran while one was open for 1% -> 1% of each run, Pallas kernels for 0% -> 0%
where the time goes in v2:
time: 156 us; the launch traced here: 155 us
  Pallas kernels  111 us (71%)
  waiting for transfers between devices  15.3 us (10%)
  local copies, waits for them, and re-layouts  14.5 us (9%)
  starting transfers between devices  12.5 us (8%)
    pallas_call x1, Pallas kernels, on_device(): pl.pallas_call(main_kernel, grid=(samples,), in_specs=[pl.BlockSpec(memor...  63.6 us
    pallas_call x1, Pallas kernels, sum_all(): pl.pallas_call(sum_kernel, in_specs=[pl.BlockSpec(memory_space=pltpu.VMEM...  33.9 us
    ppermute x4, waiting for transfers between devices, shifted(): return lax.ppermute(block, axis, route)  15.3 us
    pallas_call x1, Pallas kernels, on_device(): pl.pallas_call(tail_kernel, grid=(samples,), in_specs=[per_sample(rows, w...  13.1 us
    ppermute x4, starting transfers between devices, shifted(): return lax.ppermute(block, axis, route)  12.5 us
    unnamed x14, local copies, waits for them, and re-layouts  10.7 us
  transfers between devices with their start and end apart: 4, of which 3 were waited for; matrix products, arithmetic and copies ran while one was open for 1% of the time, Pallas kernels for 0%

profile of v2, /device:TPU:0, one launch (start us, length us, event | category | flops | bytes accessed | tf_op | source)
XLA Modules:
  0.0 155.0 jit_solution(18240259940074929088)
XLA Ops:
  0.6 1.0 fusion.1
  1.7 1.3 collective-permute-start.1
  3.0 5.5 %collective-permute-start = (bf16[12,48,128]{2,1,0:T(8,128)(2,1)S(1)}, bf16[12,48,128]{2,1,0:T(8,128)(2,1)S(1)}, u32[]{:S(2)}, u32[]{:S(2)}) collective-permute-start(bf16[12,48,128]{2,1,0:T(8,128)(2,1)S(1)} %get-tuple-element.51), channel_id=1, source_target_pairs={{0,4},{4,8},{8,12},{12,16},{16,20},{20,24},{24,28},{1,5},{5,9},{9,... | collective-permute-start | bytes 442376 | tf_op jit(solution)/shard_map/ppermute | solution.py:521
  8.5 0.8 broadcast_multiply_fusion
  9.3 0.9 mul.20.wsm_ref
  10.2 0.2 collective-permute-done.1.high_ref
  10.4 3.3 %collective-permute-done.low_ref = bf16[12,48,128]{2,1,0:T(8,128)(2,1)S(1)} collective-permute-done((bf16[12,48,128]{2,1,0:T(8,128)(2,1)S(1)}, bf16[12,48,128]{2,1,0:T(8,128)(2,1)S(1)}, u32[]{:S(2)}, u32[]{:S(2)}) %collective-permute-start) | collective-permute-done | bytes 147488 | tf_op jit(solution)/shard_map/ppermute | solution.py:521
  13.7 0.7 copy-done.3
  14.4 63.6 %shard_map.204 = (bf16[12,48,768]{2,1,0:T(8,128)(2,1)}, bf16[12,512,128]{2,1,0:T(8,128)(2,1)}, bf16[12,512,128]{2,1,0:T(8,128)(2,1)}, bf16[12,512,256]{2,1,0:T(8...) custom-call(s32[8]{0:T(128)} %counts_ref.1, ...), custom_call_target="tpu_custom_call" | custom-call | tf_op jit(solution)/shard_map/pallas_call | solution.py:557
  78.0 4.4 %collective-permute-start.2 = (bf16[12,48,256]{2,1,0:T(8,128)(2,1)}, bf16[12,48,256]{2,1,0:T(8,128)(2,1)S(1)}, u32[]{:S(2)}, u32[]{:S(2)}) collective-permute-start(bf16[12,48,256]{2,1,0:T(8,128)(2,1)} %get-tuple-element.34), channel_id=1, source_target_pairs={{0,4},{4,8},{8,12},{12,16},{16,20},{20,24},{24,28},{1,5},{5,9},{9,... | collective-permute-start | bytes 884744 | tf_op jit(solution)/shard_map/ppermute | solution.py:521
  82.4 1.3 collective-permute-start.3
  83.7 11.8 %collective-permute-done.2.low_ref = bf16[12,48,256]{2,1,0:T(8,128)(2,1)S(1)} collective-permute-done((bf16[12,48,256]{2,1,0:T(8,128)(2,1)}, bf16[12,48,256]{2,1,0:T(8,128)(2,1)S(1)}, u32[]{:S(2)}, u32[]{:S(2)}) %collective-permute-start.2) | collective-permute-done | bytes 294944 | tf_op jit(solution)/shard_map/ppermute | solution.py:521
  95.4 0.7 copy-done
  96.3 13.1 %shard_map.205 = (bf16[12,512,128]{2,1,0:T(8,128)(2,1)}, f32[1,128]{1,0:T(1,128)}, f32[128,512]{1,0:T(8,128)}) custom-call(bf16[12,512,128]{2,1,0:T(8,128)(2,1)} %atoms_ref.3, f32[1,128]{1,0:T(1,128)} %bitcast.13, bf16[128,128]{1,0:T(8,128)(2,1)} %wq_ref.3, bf16[128,128]{1,0:T(8,128)(2,1)} %wk_ref.3, bf16[128,128]{1,0:T(8,128)(2,1)} %wv_ref.3, ...), custom_call_target="tpu_custom_call" | custom-call | tf_op jit(solution)/shard_map/pallas_call | solution.py:639
  109.4 33.9 %shard_map.206 = (f32[128,128]{1,0:T(8,128)}, f32[128,128]{1,0:T(8,128)}, f32[128,128]{1,0:T(8,128)}, f32[128,128]{1,0:T(8,128)}, f32[128,128]{1,0:T(8,128)}, /*index=5*/f32[128,768]{1,0:T(8,128)}, f32[16,128]{1,0:T(8,128)}) custom-call(f32[128,128]{1,0:T(8,128)} %get-tuple-element.38.gout_ref, f32[128,768]{1,0:T(8,128)} %get-tuple-element.39.gtok_ref, ...), custom_call_target="tpu_custom_call" | custom-call | tf_op jit(solution)/shard_map/pallas_call | solution.py:492
  143.3 1.2 slice_bitcast_fusion
  144.5 0.7 slice.15
  145.2 0.6 reduce_sum.9
  145.8 1.5 copy.29
  147.3 1.5 copy.30
  148.8 1.5 copy.31
  150.3 1.5 copy.32
  151.7 1.5 copy.33
  153.2 1.8 %copy.34 = f32[128,768]{1,0:T(8,128)} copy(f32[128,768]{1,0:T(8,128)} %get-tuple-element.70) | data formatting | bytes 786432
  (9 shorter events, 0.2 us)
Async XLA Ops:
  1.7 8.7 %collective-permute-start.1 = (bf16[12,48,128]{2,1,0:T(8,128)(2,1)S(1)}, bf16[12,48,128]{2,1,0:T(8,128)(2,1)S(1)}, u32[]{:S(2)}, u32[]{:S(2)}) collective-permute-start(bf16[12,48,128]{2,1,0:T(8,128)(2,1)S(1)} %get-tuple-element.50), channel_id=1, source_target_pairs={{4,0},{8,4},{12,8},{16,12},{20,16},{24,20},{28,24},{5,1},{9,5},{13... | collective-permute-start | bytes 442376 | tf_op jit(solution)/shard_map/ppermute | solution.py:521
  3.0 10.8 %collective-permute-start = (bf16[12,48,128]{2,1,0:T(8,128)(2,1)S(1)}, bf16[12,48,128]{2,1,0:T(8,128)(2,1)S(1)}, u32[]{:S(2)}, u32[]{:S(2)}) collective-permute-start(bf16[12,48,128]{2,1,0:T(8,128)(2,1)S(1)} %get-tuple-element.51), channel_id=1, source_target_pairs={{0,4},{4,8},{8,12},{12,16},{16,20},{20,24},{24,28},{1,5},{5,9},{9,... | collective-permute-start | bytes 442376 | tf_op jit(solution)/shard_map/ppermute | solution.py:521
  10.4 3.3 %copy-start.2 = (bf16[12,48,128]{2,1,0:T(8,128)(2,1)}, bf16[12,48,128]{2,1,0:T(8,128)(2,1)S(1)}, u32[]{:S(2)}) copy-start(bf16[12,48,128]{2,1,0:T(8,128)(2,1)S(1)} %collective-permute-done.1.high_ref) | copy-start | bytes 442372
  13.7 0.7 copy-start.3
  78.0 17.5 %collective-permute-start.2 = (bf16[12,48,256]{2,1,0:T(8,128)(2,1)}, bf16[12,48,256]{2,1,0:T(8,128)(2,1)S(1)}, u32[]{:S(2)}, u32[]{:S(2)}) collective-permute-start(bf16[12,48,256]{2,1,0:T(8,128)(2,1)} %get-tuple-element.34), channel_id=1, source_target_pairs={{0,4},{4,8},{8,12},{12,16},{16,20},{20,24},{24,28},{1,5},{5,9},{9,... | collective-permute-start | bytes 884744 | tf_op jit(solution)/shard_map/ppermute | solution.py:521
  82.4 13.1 %collective-permute-start.3 = (bf16[12,48,256]{2,1,0:T(8,128)(2,1)}, bf16[12,48,256]{2,1,0:T(8,128)(2,1)S(1)}, u32[]{:S(2)}, u32[]{:S(2)}) collective-permute-start(bf16[12,48,256]{2,1,0:T(8,128)(2,1)} %get-tuple-element.35), channel_id=1, source_target_pairs={{4,0},{8,4},{12,8},{16,12},{20,16},{24,20},{28,24},{5,1},{9,5},{13... | collective-permute-start | bytes 884744 | tf_op jit(solution)/shard_map/ppermute | solution.py:521
  95.4 0.7 copy-start
  95.4 0.9 copy-start.1

commit v3 on v2

--- a/solution.py
+++ b/solution.py
@@ -375,29 +375,23 @@
     return bits
 
 
-def sum_kernel(
-    gout_ref,
-    gtok_ref,
-    gw_ref,
-    rsum_ref,
-    ggain_ref,
-    gq_out,
-    gk_out,
-    gv_out,
-    gg_out,
-    gout_out,
-    gtok_out,
-    small_out,
-    buf,
-    gbuf,
-    send_sem,
-    recv_sem,
-    *slots,
-):
+def sum_kernel(parts, streams, *refs):
+    grads = refs[: 5 * parts]
+    out_ref, buf, send_sem, recv_sem = refs[5 * parts : 5 * parts + 4]
+    slots = refs[5 * parts + 4 :]
+
+    def total(n, *at):
+        value = grads[n][at] if at else grads[n][...]
+        for p in range(1, parts):
+            more = grads[5 * p + n]
+            value = value + (more[at] if at else more[...])
+        return value
+
+    gtok_ref, rsum_ref = grads[1], grads[3]
+    width = grads[0].shape[0]
     bits = axis_bits()
     count = len(bits)
-    sends, recvs = slots[:count], slots[count:]
-    width = gout_ref.shape[0]
+    sends, recvs = slots[: streams * count], slots[streams * count :]
     where = []
     for axis, bit in bits:
         me = lax.axis_index(axis)
@@ -409,21 +403,22 @@
             barrier, inc=1, device_id=partner, device_id_type=pl.DeviceIdType.MESH
         )
 
+    every = slice(None)
     blocks = gtok_ref.shape[1] // width
     for n in range(blocks):
-        buf[n * width : (n + 1) * width, :] = gtok_ref[:, n * width : (n + 1) * width]
+        buf[n * width : (n + 1) * width, :] = total(1, every, slice(n * width, (n + 1) * width))
     for n in range(4):
         at = (blocks + n) * width
-        buf[at : at + width, :] = gw_ref[:, n * width : (n + 1) * width]
+        buf[at : at + width, :] = total(2, every, slice(n * width, (n + 1) * width))
     at = (blocks + 4) * width
-    buf[at : at + width, :] = gout_ref[...]
+    buf[at : at + width, :] = total(0)
     at += width
     buf[at:, :] = jnp.zeros((buf.shape[0] - at, width), F32)
     high, wide = rsum_ref.shape
     per = high // HEADS
     row = lax.broadcasted_iota(jnp.int32, (high, wide), 0)
     lane = lax.broadcasted_iota(jnp.int32, (high, wide), 1)
-    diagonal = jnp.where(lax.rem(row, per) == lane // (wide // per), rsum_ref[...], 0.0)
+    diagonal = jnp.where(lax.rem(row, per) == lane // (wide // per), total(3), 0.0)
     for h in range(HEADS):
         line = jnp.sum(diagonal[h * per : (h + 1) * per], axis=0, keepdims=True)
         for n in range(wide // width):
@@ -431,84 +426,126 @@
                 :, n * width : (n + 1) * width
             ]
     spot = at + HEADS * (wide // width)
-    buf[spot : spot + 1, :] = ggain_ref[...]
+    buf[spot : spot + 1, :] = total(4)
     pl.semaphore_wait(barrier, count)
 
-    off = 0
-    length = buf.shape[0]
-    for k, (upper, partner) in enumerate(where):
-        length //= 2
-        keep = pl.multiple_of(off + upper * length, 16)
-        give = pl.multiple_of(off + (1 - upper) * length, 16)
-        sends[k][...] = buf[pl.ds(give, length), :].astype(BF16)
+    size = buf.shape[0] // streams
+    orders = []
+    for stream in range(streams):
+        order = list(range(count))
+        turn = (stream * 2) % 3
+        order[:3] = order[turn:3] + order[:turn]
+        orders.append(order)
+    offs = [stream * size for stream in range(streams)]
+    lengths = [size] * streams
+    pending = [None] * streams
+
+    def send(stream, src, dst, slot, partner):
         copy = pltpu.make_async_remote_copy(
-            src_ref=sends[k],
-            dst_ref=recvs[k],
-            send_sem=send_sem.at[k],
-            recv_sem=recv_sem.at[k],
+            src_ref=src,
+            dst_ref=dst,
+            send_sem=send_sem.at[stream * 2 * count + slot],
+            recv_sem=recv_sem.at[stream * 2 * count + slot],
             device_id=partner,
             device_id_type=pl.DeviceIdType.MESH,
         )
         copy.start()
-        copy.wait()
-        buf[pl.ds(keep, length), :] = buf[pl.ds(keep, length), :] + recvs[k][...].astype(F32)
-        off = keep
-    gbuf[pl.ds(off, length), :] = buf[pl.ds(off, length), :].astype(BF16)
+        pending[stream] = copy
+
+    def absorb(stream, k):
+        pending[stream].wait()
+        rows = pl.ds(offs[stream], lengths[stream])
+        buf[rows, :] = buf[rows, :] + recvs[stream * count + k][...].astype(F32)
+
+    for k in range(count):
+        for stream in range(streams):
+            if k > 0:
+                absorb(stream, k - 1)
+            upper, partner = where[orders[stream][k]]
+            lengths[stream] //= 2
+            length = lengths[stream]
+            keep = pl.multiple_of(offs[stream] + upper * length, 16)
+            give = pl.multiple_of(offs[stream] + (1 - upper) * length, 16)
+            slot = sends[stream * count + k]
+            slot[...] = buf[pl.ds(give, length), :].astype(BF16)
+            send(stream, slot, recvs[stream * count + k], k, partner)
+            offs[stream] = keep
     for k in range(count - 1, -1, -1):
-        upper, partner = where[k]
-        part = gbuf.at[pl.ds(pl.multiple_of(off, 16), length), :]
-        copy = pltpu.make_async_remote_copy(
-            src_ref=part,
-            dst_ref=part,
-            send_sem=send_sem.at[count + k],
-            recv_sem=recv_sem.at[count + k],
-            device_id=partner,
-            device_id_type=pl.DeviceIdType.MESH,
-        )
-        copy.start()
-        copy.wait()
-        off = off - upper * length
-        length *= 2
+        for stream in range(streams):
+            upper, partner = where[orders[stream][k]]
+            length = lengths[stream]
+            if k == count - 1:
+                absorb(stream, k)
+                rows = pl.ds(offs[stream], length)
+                out_ref[rows, :] = buf[rows, :].astype(BF16)
+            else:
+                pending[stream].wait()
+            part = out_ref.at[pl.ds(pl.multiple_of(offs[stream], 16), length), :]
+            send(stream, part, part, count + k, partner)
+            offs[stream] = offs[stream] - upper * length
+            lengths[stream] *= 2
+    for stream in range(streams):
+        pending[stream].wait()
+
+
+def unpack_kernel(packed_ref, gq_out, gk_out, gv_out, gg_out, gout_out, gtok_out, small_out):
+    width = gout_out.shape[0]
+    blocks = gtok_out.shape[1] // width
 
     def block(n):
-        return gbuf[n * width : (n + 1) * width, :].astype(F32)
+        return packed_ref[n * width : (n + 1) * width, :].astype(F32)
 
     for n in range(blocks):
         gtok_out[:, n * width : (n + 1) * width] = block(n)
     for n, ref in enumerate((gq_out, gk_out, gv_out, gg_out, gout_out)):
         ref[...] = block(blocks + n)
-    small_out[...] = gbuf[at : at + small_out.shape[0], :].astype(F32)
-
-
-def sum_all(gout, gtok, gw, rsum, ggain):
+    at = (blocks + 5) * width
+    small_out[...] = packed_ref[at : at + small_out.shape[0], :].astype(F32)
+
+
+def sum_all(halves):
     shape = jax.ShapeDtypeStruct
+    gout, gtok, gw = halves[0][:3]
     width = gout.shape[0]
-    bits = axis_bits()
-    count = len(bits)
+    count = len(axis_bits())
     unit = 16 * 2**count
     lines = gtok.shape[1] + gw.shape[1] + width + 16
     total = -(-lines // unit) * unit
-    slots = [pltpu.VMEM((total >> (k + 1), width), BF16) for k in range(count)]
+    streams = total // unit
+    slots = [pltpu.VMEM((unit >> (k + 1), width), BF16) for k in range(count)]
+    operands = [x for half in halves for x in half]
+    vmem = pl.BlockSpec(memory_space=pltpu.VMEM)
+    packed = pl.pallas_call(
+        functools.partial(sum_kernel, len(halves), streams),
+        in_specs=[vmem] * len(operands),
+        out_specs=vmem,
+        out_shape=shape((total, width), BF16),
+        scratch_shapes=[
+            pltpu.VMEM((total, width), F32),
+            pltpu.SemaphoreType.DMA((2 * streams * count,)),
+            pltpu.SemaphoreType.DMA((2 * streams * count,)),
+        ]
+        + slots * (2 * streams),
+        compiler_params=pltpu.CompilerParams(collective_id=0, has_side_effects=True),
+    )(*operands)
     return pl.pallas_call(
-        sum_kernel,
-        in_specs=[pl.BlockSpec(memory_space=pltpu.VMEM)] * 5,
-        out_specs=[pl.BlockSpec(memory_space=pltpu.VMEM)] * 7,
+        unpack_kernel,
+        in_specs=[vmem],
+        out_specs=[vmem] * 7,
         out_shape=[shape((width, width), F32)] * 5
         + [shape(gtok.shape, F32), shape((16, width), F32)],
-        scratch_shapes=[
-            pltpu.VMEM((total, width), F32),
-            pltpu.VMEM((total, width), BF16),
-            pltpu.SemaphoreType.DMA((2 * count,)),
-            pltpu.SemaphoreType.DMA((2 * count,)),
-        ]
-        + slots
-        + slots,
-        compiler_params=pltpu.CompilerParams(collective_id=0, has_side_effects=True),
-    )(gout, gtok, gw, rsum, ggain)
-
-
-def per_sample(*shape):
-    return pl.BlockSpec((1,) + shape, lambda s: (s,) + (0,) * len(shape))
+    )(packed)
+
+
+def per_sample(*shape, base=0):
+    return pl.BlockSpec((1,) + shape, lambda s: (s + base,) + (0,) * len(shape))
+
+
+def dropping(kernel, position):
+    def body(*refs):
+        return kernel(*refs[:position], *refs[position + 1 :])
+
+    return body
 
 
 def whole(*shape):
@@ -542,24 +579,23 @@
     tokens, token_width = pooled_cot.shape[1:]
     channels = w_pair.shape[0]
     per = 2 * LANES // channels
-    low = shifted(atoms[:, rows - rim :], "seq", 1)
-    high = shifted(atoms[:, :rim], "seq", -1)
     wsm = (
         w_pair.T[:, None, None, :] * jnp.eye(per, dtype=BF16)[None, :, :, None]
     ).reshape(HEADS * per, per * channels)
     pair2 = pair_cond.reshape(blocks * QBLK, pair_cond.shape[-1])
     gain2 = gain.reshape(1, width)
+    ids2 = membership.reshape(1, rows)
     square = whole(width, width)
     params = pltpu.CompilerParams(
         dimension_semantics=("arbitrary",), vmem_limit_bytes=56 * 1024 * 1024
     )
     shape = jax.ShapeDtypeStruct
-    (pooled, gupd, dq, dkv, edge_low, edge_high, dg, gout, gtok, rsum) = pl.pallas_call(
-        main_kernel,
-        grid=(samples,),
-        in_specs=[
+    anywhere = pl.BlockSpec(memory_space=pl.ANY)
+
+    def run_main(base, count, low, high, before):
+        specs = [
             pl.BlockSpec(memory_space=pltpu.SMEM),
-            per_sample(rows, width),
+            per_sample(rows, width, base=base),
             per_sample(rim, width),
             per_sample(rim, width),
             whole(1, width),
@@ -572,113 +608,156 @@
             whole(*wsm.shape),
             whole(*pair2.shape),
             whole(1, rows),
-            per_sample(tokens, token_width),
-        ],
-        out_specs=[
-            per_sample(tokens, token_width),
-            per_sample(rows, width),
-            per_sample(rows, width),
-            per_sample(rows, 2 * width),
-            per_sample(rim, 2 * width),
-            per_sample(rim, 2 * width),
-            per_sample(rows, width),
-            square,
-            whole(width, token_width),
-            whole(*wsm.shape),
-        ],
-        out_shape=[
-            shape((samples, tokens, token_width), BF16),
-            shape((samples, rows, width), BF16),
-            shape((samples, rows, width), BF16),
-            shape((samples, rows, 2 * width), BF16),
-            shape((samples, rim, 2 * width), BF16),
-            shape((samples, rim, 2 * width), BF16),
-            shape((samples, rows, width), BF16),
-            shape((width, width), F32),
-            shape((width, token_width), F32),
-            shape(wsm.shape, F32),
-        ],
-        scratch_shapes=[
-            pltpu.VMEM((blocks, KWIN, LANES), F32),
-            pltpu.VMEM((blocks, KWIN, LANES), F32),
-            pltpu.VMEM((rows, tokens), BF16),
-            pltpu.VMEM((tokens, rows), BF16),
-            pltpu.VMEM((tokens, 1), F32),
-            pltpu.VMEM((width, 2 * width), BF16),
-            pltpu.VMEM((width, 2 * width), BF16),
-            pltpu.VMEM((rows + 2 * rim, width), BF16),
-            pltpu.VMEM((rows, width), BF16),
-            pltpu.VMEM((rows, width), F32),
-            pltpu.VMEM((rows + 2 * rim, 2 * width), BF16),
-            pltpu.VMEM((blocks, KWIN, LANES), F32),
-            pltpu.VMEM((blocks, KWIN, LANES), BF16),
-            pltpu.VMEM((rows, width), F32),
-            pltpu.VMEM((rows, width), BF16),
-            pltpu.VMEM((rows + 2 * rim, 2 * width), F32),
-        ],
-        compiler_params=params,
-    )(
-        counts,
-        atoms,
-        low,
-        high,
-        gain2,
-        w_query,
-        w_key,
-        w_value,
-        w_gate,
-        w_out,
-        w_token,
-        wsm,
-        pair2,
-        membership.reshape(1, rows),
-        pooled_cot,
-    )
-    from_left = shifted(edge_high, "seq", 1)
-    from_right = shifted(edge_low, "seq", -1)
-    grad_atoms, ggain, gw = pl.pallas_call(
-        tail_kernel,
-        grid=(samples,),
-        in_specs=[
-            per_sample(rows, width),
-            whole(1, width),
-            square,
-            square,
-            square,
-            square,
-            per_sample(rows, width),
-            per_sample(rows, width),
-            per_sample(rows, 2 * width),
-            per_sample(rim, 2 * width),
-            per_sample(rim, 2 * width),
-            per_sample(rows, width),
-        ],
-        out_specs=[per_sample(rows, width), whole(1, width), whole(width, 4 * width)],
-        out_shape=[
-            shape((samples, rows, width), BF16),
-            shape((1, width), F32),
-            shape((width, 4 * width), F32),
-        ],
-        scratch_shapes=[
-            pltpu.VMEM((rows, 4 * width), BF16),
-            pltpu.VMEM((width, 4 * width), BF16),
-        ],
-        compiler_params=params,
-    )(
-        atoms,
-        gain2,
-        w_query,
-        w_key,
-        w_value,
-        w_gate,
-        gupd,
-        dq,
-        dkv,
-        from_left,
-        from_right,
-        dg,
-    )
-    gq, gk, gv, gg, gout, gtok, small = sum_all(gout, gtok, gw, rsum, ggain)
+            per_sample(tokens, token_width, base=base),
+        ]
+        operands = [
+            counts,
+            atoms,
+            low,
+            high,
+            gain2,
+            w_query,
+            w_key,
+            w_value,
+            w_gate,
+            w_out,
+            w_token,
+            wsm,
+            pair2,
+            ids2,
+            pooled_cot,
+        ]
+        place = len(operands)
+        return pl.pallas_call(
+            main_kernel if before is None else dropping(main_kernel, place),
+            grid=(count,),
+            in_specs=specs + ([] if before is None else [anywhere]),
+            out_specs=[
+                per_sample(tokens, token_width, base=base),
+                per_sample(rows, width),
+                per_sample(rows, width),
+                per_sample(rows, 2 * width),
+                per_sample(rim, 2 * width),
+                per_sample(rim, 2 * width),
+                per_sample(rows, width),
+                square,
+                whole(width, token_width),
+                whole(*wsm.shape),
+            ],
+            out_shape=[
+                shape((samples, tokens, token_width), BF16),
+                shape((count, rows, width), BF16),
+                shape((count, rows, width), BF16),
+                shape((count, rows, 2 * width), BF16),
+                shape((count, rim, 2 * width), BF16),
+                shape((count, rim, 2 * width), BF16),
+                shape((count, rows, width), BF16),
+                shape((width, width), F32),
+                shape((width, token_width), F32),
+                shape(wsm.shape, F32),
+            ],
+            scratch_shapes=[
+                pltpu.VMEM((blocks, KWIN, LANES), F32),
+                pltpu.VMEM((blocks, KWIN, LANES), F32),
+                pltpu.VMEM((rows, tokens), BF16),
+                pltpu.VMEM((tokens, rows), BF16),
+                pltpu.VMEM((tokens, 1), F32),
+                pltpu.VMEM((width, 2 * width), BF16),
+                pltpu.VMEM((width, 2 * width), BF16),
+                pltpu.VMEM((rows + 2 * rim, width), BF16),
+                pltpu.VMEM((rows, width), BF16),
+                pltpu.VMEM((rows, width), F32),
+                pltpu.VMEM((rows + 2 * rim, 2 * width), BF16),
+                pltpu.VMEM((blocks, KWIN, LANES), F32),
+                pltpu.VMEM((blocks, KWIN, LANES), BF16),
+                pltpu.VMEM((rows, width), F32),
+                pltpu.VMEM((rows, width), BF16),
+                pltpu.VMEM((rows + 2 * rim, 2 * width), F32),
+            ],
+            input_output_aliases={} if before is None else {place: 0},
+            cost_estimate=pl.CostEstimate(
+                flops=count * rows * 4000000, bytes_accessed=1 << 22, transcendentals=0
+            ),
+            compiler_params=params,
+        )(*operands, *([] if before is None else [before]))
+
+    def run_tail(base, count, gupd, dq, dkv, from_left, from_right, dg, before):
+        operands = [
+            atoms,
+            gain2,
+            w_query,
+            w_key,
+            w_value,
+            w_gate,
+            gupd,
+            dq,
+            dkv,
+            from_left,
+            from_right,
+            dg,
+        ]
+        place = len(operands)
+        return pl.pallas_call(
+            tail_kernel if before is None else dropping(tail_kernel, place),
+            grid=(count,),
+            in_specs=[
+                per_sample(rows, width, base=base),
+                whole(1, width),
+                square,
+                square,
+                square,
+                square,
+                per_sample(rows, width),
+                per_sample(rows, width),
+                per_sample(rows, 2 * width),
+                per_sample(rim, 2 * width),
+                per_sample(rim, 2 * width),
+                per_sample(rows, width),
+            ]
+            + ([] if before is None else [anywhere]),
+            out_specs=[
+                per_sample(rows, width, base=base),
+                whole(1, width),
+                whole(width, 4 * width),
+            ],
+            out_shape=[
+                shape((samples, rows, width), BF16),
+                shape((1, width), F32),
+                shape((width, 4 * width), F32),
+            ],
+            scratch_shapes=[
+                pltpu.VMEM((rows, 4 * width), BF16),
+                pltpu.VMEM((width, 4 * width), BF16),
+            ],
+            input_output_aliases={} if before is None else {place: 0},
+            cost_estimate=pl.CostEstimate(
+                flops=count * rows * 800000, bytes_accessed=1 << 22, transcendentals=0
+            ),
+            compiler_params=params,
+        )(*operands, *([] if before is None else [before]))
+
+    first = samples // 2
+    cuts = [(0, first), (first, samples - first)]
+    rims = []
+    for base, count in cuts:
+        low = shifted(atoms[base : base + count, rows - rim :], "seq", 1)
+        high = shifted(atoms[base : base + count, :rim], "seq", -1)
+        rims.append((low, high))
+    pooled = None
+    mains = []
+    for (base, count), (low, high) in zip(cuts, rims):
+        outs = run_main(base, count, low, high, pooled)
+        pooled = outs[0]
+        _, gupd, dq, dkv, edge_low, edge_high, dg, gout, gtok, rsum = outs
+        from_left = shifted(edge_high, "seq", 1)
+        from_right = shifted(edge_low, "seq", -1)
+        mains.append((gupd, dq, dkv, from_left, from_right, dg, gout, gtok, rsum))
+    grad_atoms = None
+    sums = []
+    for (base, count), (*moved, gout, gtok, rsum) in zip(cuts, mains):
+        grad_atoms, ggain, gw = run_tail(base, count, *moved, grad_atoms)
+        sums.append((gout, gtok, gw, rsum, ggain))
+    gq, gk, gv, gg, gout, gtok, small = sum_all(sums)
     halves = rsum.shape[1] // width
     lines = small[: halves * HEADS].reshape(halves, HEADS, width // channels, channels)
     gpair = jnp.sum(lines, axis=(0, 2)).T

time: 156 us -> 155 us (level)
  waiting for transfers between devices: 15.3 us -> 0.02 us
  starting transfers between devices: 12.5 us -> 25.7 us
  Pallas kernels: 111 us -> 120 us
  local copies, waits for them, and re-layouts: 14.5 us -> 6.49 us
    ppermute x4 -> x8, waiting for transfers between devices: 15.3 us -> 0.02 us  [shifted(): return lax.ppermute(block, axis, route)]
    ppermute x4 -> x8, starting transfers between devices: 12.5 us -> 25.7 us  [shifted(): return lax.ppermute(block, axis, route)]
    pallas_call x3 -> x6, Pallas kernels: 111 us -> 120 us  [the longest x2 68.8 us: run_main(): pl.pallas_call(main_kernel if before is None else dropping(main_kernel, p...]
    unnamed x14 -> x16, local copies, waits for them, and re-layouts: 10.7 us -> 2.68 us
  transfers between devices with their start and end apart: 4 -> 8, of which waited for: 3 -> 0; matrix products, arithmetic and copies ran while one was open for 1% -> 1% of each run, Pallas kernels for 0% -> 49%
where the time goes in v3:
time: 155 us; the launch traced here: 154 us
  Pallas kernels  120 us (77%)
  starting transfers between devices  25.7 us (17%)
  local copies, waits for them, and re-layouts  6.49 us (4%)
    pallas_call x2, Pallas kernels, run_main(): pl.pallas_call(main_kernel if before is None else dropping(main_kernel, p...  68.8 us
    pallas_call x1, Pallas kernels, sum_all(): pl.pallas_call(functools.partial(sum_kernel, len(halves), streams), in_sp...  34.5 us
    ppermute x8, starting transfers between devices, shifted(): return lax.ppermute(block, axis, route)  25.7 us
    pallas_call x2, Pallas kernels, run_tail(): pl.pallas_call(tail_kernel if before is None else dropping(tail_kernel, p...  14.6 us
  transfers between devices with their start and end apart: 8, of which 0 were waited for; matrix products, arithmetic and copies ran while one was open for 1% of the time, Pallas kernels for 49%

profile of v3, /device:TPU:0, one launch (start us, length us, event | category | flops | bytes accessed | tf_op | source)
XLA Modules:
  0.0 154.2 jit_solution(10834462211539750505)
XLA Ops:
  0.6 1.0 fusion.1
  1.7 1.3 collective-permute-start.3
  3.0 5.5 %collective-permute-start.2 = (bf16[6,48,128]{2,1,0:T(8,128)(2,1)S(1)}, bf16[6,48,128]{2,1,0:T(8,128)(2,1)S(1)}, u32[]{:S(2)}, u32[]{:S(2)}) collective-permute-start(bf16[6,48,128]{2,1,0:T(8,128)(2,1)S(1)} %get-tuple-element.77), channel_id=1, source_target_pairs={{0,4},{4,8},{8,12},{12,16},{16,20},{20,24},{24,28},{1,5},{5,9},{9,... | collective-permute-start | bytes 221192 | tf_op jit(solution)/shard_map/ppermute | solution.py:558
  8.5 1.3 collective-permute-start.1
  9.8 5.4 %collective-permute-start = (bf16[6,48,128]{2,1,0:T(8,128)(2,1)S(1)}, bf16[6,48,128]{2,1,0:T(8,128)(2,1)S(1)}, u32[]{:S(2)}, u32[]{:S(2)}) collective-permute-start(bf16[6,48,128]{2,1,0:T(8,128)(2,1)S(1)} %get-tuple-element.79), channel_id=1, source_target_pairs={{0,4},{4,8},{8,12},{12,16},{16,20},{20,24},{24,28},{1,5},{5,9},{9,... | collective-permute-start | bytes 221192 | tf_op jit(solution)/shard_map/ppermute | solution.py:558
  15.3 0.8 broadcast_multiply_fusion
  16.1 0.9 mul.20.wsm_ref.refs_11_
  16.9 0.6 copy-done.6
  17.6 34.3 %shard_map.204 = (bf16[12,48,768]{2,1,0:T(8,128)(2,1)}, bf16[6,512,128]{2,1,0:T(8,128)(2,1)}, bf16[6,512,128]{2,1,0:T(8,128)(2,1)}, bf16[6,512,256]{2,1,0:T(8,12...) custom-call(s32[8]{0:T(128)} %refs_0_.2, ...), custom_call_target="tpu_custom_call" | custom-call | flops 12288000000 | bytes 4194304 | tf_op jit(solution)/shard_map/pallas_call | solution.py:631
  51.9 4.8 %collective-permute-start.6 = (bf16[6,48,256]{2,1,0:T(8,128)(2,1)}, bf16[6,48,256]{2,1,0:T(8,128)(2,1)S(1)}, u32[]{:S(2)}, u32[]{:S(2)}) collective-permute-start(bf16[6,48,256]{2,1,0:T(8,128)(2,1)} %get-tuple-element.54), channel_id=1, source_target_pairs={{0,4},{4,8},{8,12},{12,16},{16,20},{20,24},{24,28},{1,5},{5,9},{9,... | collective-permute-start | bytes 442376 | tf_op jit(solution)/shard_map/ppermute | solution.py:558
  56.8 1.5 collective-permute-start.7
  58.3 0.6 copy-done.4
  58.9 34.4 %shard_map.205 = (bf16[12,48,768]{2,1,0:T(8,128)(2,1)}, bf16[6,512,128]{2,1,0:T(8,128)(2,1)}, bf16[6,512,128]{2,1,0:T(8,128)(2,1)}, bf16[6,512,256]{2,1,0:T(8,12...) custom-call(s32[8]{0:T(128)} %refs_0_.2, ...), custom_call_target="tpu_custom_call", output_to_operand_aliasing={{0}: (15, {})} | custom-call | flops 12288000000 | bytes 4194304 | tf_op jit(solution)/shard_map/pallas_call | solution.py:631
  93.3 4.6 %collective-permute-start.4 = (bf16[6,48,256]{2,1,0:T(8,128)(2,1)}, bf16[6,48,256]{2,1,0:T(8,128)(2,1)S(1)}, u32[]{:S(2)}, u32[]{:S(2)}) collective-permute-start(bf16[6,48,256]{2,1,0:T(8,128)(2,1)} %get-tuple-element.48), channel_id=1, source_target_pairs={{0,4},{4,8},{8,12},{12,16},{16,20},{20,24},{24,28},{1,5},{5,9},{9,... | collective-permute-start | bytes 442376 | tf_op jit(solution)/shard_map/ppermute | solution.py:558
  97.9 1.3 collective-permute-start.5
  99.2 0.6 copy-done
  100.0 7.3 %shard_map.206 = (bf16[12,512,128]{2,1,0:T(8,128)(2,1)}, f32[1,128]{1,0:T(1,128)}, f32[128,512]{1,0:T(8,128)}) custom-call(bf16[12,512,128]{2,1,0:T(8,128)(2,1)} %refs_0_.3, f32[1,128]{1,0:T(1,128)} %bitcast.17, bf16[128,128]{1,0:T(8,128)(2,1)} %refs_2_.1, bf16[128,128]{1,0:T(8,128)(2,1)} %refs_3_.1, bf16[128,128]{1,0:T(8,128)(2,1)} %refs_4_.1, ...), custom_call_target="tpu_custom_call" | custom-call | flops 2457600000 | bytes 4194304 | tf_op jit(solution)/shard_map/pallas_call | solution.py:700
  107.3 0.6 copy-done.2
  108.0 7.3 %shard_map.207 = (bf16[12,512,128]{2,1,0:T(8,128)(2,1)}, f32[1,128]{1,0:T(1,128)}, f32[128,512]{1,0:T(8,128)}) custom-call(bf16[12,512,128]{2,1,0:T(8,128)(2,1)} %refs_0_.3, f32[1,128]{1,0:T(1,128)} %bitcast.18, bf16[128,128]{1,0:T(8,128)(2,1)} %refs_2_.1, bf16[128,128]{1,0:T(8,128)(2,1)} %refs_3_.1, ...), custom_call_target="tpu_custom_call", output_to_operand_aliasing={{0}: (12, {})} | custom-call | flops 2457600000 | bytes 4194304 | tf_op jit(solution)/shard_map/pallas_call | solution.py:700
  115.3 34.5 %shard_map.208.packed_ref = bf16[1536,128]{1,0:T(8,128)(2,1)} custom-call(f32[128,128]{1,0:T(8,128)} %get-tuple-element.59.refs_0_, f32[128,768]{1,0:T(8,128)} %get-tuple-element.60.refs_1_, f32[128,512]{1,0:T(8,128)} %get-tuple-element.61.refs_2_, f32[64,256]{1,0:T(8,128)} %get-tuple-element.62.refs_3_, f32[1,128]{1,0:T(1,128)} %get-tuple-element.63.refs_4_, ...), custom_call_target="tpu_custom_call" | custom-call | tf_op jit(solution)/shard_map/pallas_call | solution.py:518
  149.7 1.9 %shard_map.209 = (f32[128,128]{1,0:T(8,128)}, f32[128,128]{1,0:T(8,128)}, f32[128,128]{1,0:T(8,128)}, f32[128,128]{1,0:T(8,128)}, f32[128,128]{1,0:T(8,128)}, /*index=5*/f32[128,768]{1,0:T(8,128)}, f32[16,128]{1,0:T(8,128)}) custom-call(bf16[1536,128]{1,0:T(8,128)(2,1)} %shard_map.208.packed_ref), custom_call_target="tpu_custom_call" | custom-call | tf_op jit(solution)/shard_map/pallas_call | solution.py:531
  151.6 1.2 slice_bitcast_fusion
  152.8 0.7 slice.23
  153.6 0.6 reduce_sum.9
  (22 shorter events, 0.3 us)
Async XLA Ops:
  1.7 15.3 %collective-permute-start.3 = (bf16[6,48,128]{2,1,0:T(8,128)(2,1)S(1)}, bf16[6,48,128]{2,1,0:T(8,128)(2,1)S(1)}, u32[]{:S(2)}, u32[]{:S(2)}) collective-permute-start(bf16[6,48,128]{2,1,0:T(8,128)(2,1)S(1)} %get-tuple-element.76), channel_id=1, source_target_pairs={{4,0},{8,4},{12,8},{16,12},{20,16},{24,20},{28,24},{5,1},{9,5},{13... | collective-permute-start | bytes 221192 | tf_op jit(solution)/shard_map/ppermute | solution.py:558
  3.0 14.0 %collective-permute-start.2 = (bf16[6,48,128]{2,1,0:T(8,128)(2,1)S(1)}, bf16[6,48,128]{2,1,0:T(8,128)(2,1)S(1)}, u32[]{:S(2)}, u32[]{:S(2)}) collective-permute-start(bf16[6,48,128]{2,1,0:T(8,128)(2,1)S(1)} %get-tuple-element.77), channel_id=1, source_target_pairs={{0,4},{4,8},{8,12},{12,16},{16,20},{20,24},{24,28},{1,5},{5,9},{9,... | collective-permute-start | bytes 221192 | tf_op jit(solution)/shard_map/ppermute | solution.py:558
  8.5 49.8 %collective-permute-start.1 = (bf16[6,48,128]{2,1,0:T(8,128)(2,1)S(1)}, bf16[6,48,128]{2,1,0:T(8,128)(2,1)S(1)}, u32[]{:S(2)}, u32[]{:S(2)}) collective-permute-start(bf16[6,48,128]{2,1,0:T(8,128)(2,1)S(1)} %get-tuple-element.78), channel_id=1, source_target_pairs={{4,0},{8,4},{12,8},{16,12},{20,16},{24,20},{28,24},{5,1},{9,5},{13... | collective-permute-start | bytes 221192 | tf_op jit(solution)/shard_map/ppermute | solution.py:558
  9.8 48.5 %collective-permute-start = (bf16[6,48,128]{2,1,0:T(8,128)(2,1)S(1)}, bf16[6,48,128]{2,1,0:T(8,128)(2,1)S(1)}, u32[]{:S(2)}, u32[]{:S(2)}) collective-permute-start(bf16[6,48,128]{2,1,0:T(8,128)(2,1)S(1)} %get-tuple-element.79), channel_id=1, source_target_pairs={{0,4},{4,8},{8,12},{12,16},{16,20},{20,24},{24,28},{1,5},{5,9},{9,... | collective-permute-start | bytes 221192 | tf_op jit(solution)/shard_map/ppermute | solution.py:558
  16.9 0.7 copy-start.6
  16.9 0.7 copy-start.7
  51.9 47.3 %collective-permute-start.6 = (bf16[6,48,256]{2,1,0:T(8,128)(2,1)}, bf16[6,48,256]{2,1,0:T(8,128)(2,1)S(1)}, u32[]{:S(2)}, u32[]{:S(2)}) collective-permute-start(bf16[6,48,256]{2,1,0:T(8,128)(2,1)} %get-tuple-element.54), channel_id=1, source_target_pairs={{0,4},{4,8},{8,12},{12,16},{16,20},{20,24},{24,28},{1,5},{5,9},{9,... | collective-permute-start | bytes 442376 | tf_op jit(solution)/shard_map/ppermute | solution.py:558
  56.8 42.4 %collective-permute-start.7 = (bf16[6,48,256]{2,1,0:T(8,128)(2,1)}, bf16[6,48,256]{2,1,0:T(8,128)(2,1)S(1)}, u32[]{:S(2)}, u32[]{:S(2)}) collective-permute-start(bf16[6,48,256]{2,1,0:T(8,128)(2,1)} %get-tuple-element.55), channel_id=1, source_target_pairs={{4,0},{8,4},{12,8},{16,12},{20,16},{24,20},{28,24},{5,1},{9,5},{13... | collective-permute-start | bytes 442376 | tf_op jit(solution)/shard_map/ppermute | solution.py:558
  58.3 0.6 copy-start.4
  58.3 0.6 copy-start.5
  93.3 13.9 %collective-permute-start.4 = (bf16[6,48,256]{2,1,0:T(8,128)(2,1)}, bf16[6,48,256]{2,1,0:T(8,128)(2,1)S(1)}, u32[]{:S(2)}, u32[]{:S(2)}) collective-permute-start(bf16[6,48,256]{2,1,0:T(8,128)(2,1)} %get-tuple-element.48), channel_id=1, source_target_pairs={{0,4},{4,8},{8,12},{12,16},{16,20},{20,24},{24,28},{1,5},{5,9},{9,... | collective-permute-start | bytes 442376 | tf_op jit(solution)/shard_map/ppermute | solution.py:558
  97.9 9.4 %collective-permute-start.5 = (bf16[6,48,256]{2,1,0:T(8,128)(2,1)}, bf16[6,48,256]{2,1,0:T(8,128)(2,1)S(1)}, u32[]{:S(2)}, u32[]{:S(2)}) collective-permute-start(bf16[6,48,256]{2,1,0:T(8,128)(2,1)} %get-tuple-element.49), channel_id=1, source_target_pairs={{4,0},{8,4},{12,8},{16,12},{20,16},{24,20},{28,24},{5,1},{9,5},{13... | collective-permute-start | bytes 442376 | tf_op jit(solution)/shard_map/ppermute | solution.py:558
  99.2 0.7 copy-start
  99.2 0.7 copy-start.1
  107.2 0.7 copy-start.2
  107.3 0.7 copy-start.3

commit v4 on v3

--- a/solution.py
+++ b/solution.py
@@ -365,14 +365,8 @@
     gatoms_ref[0] = (gupd_ref[0].astype(F32) + grad_ln).astype(BF16)
 
 
-def axis_bits():
-    bits = []
-    for axis in ("samp", "seq"):
-        bit = 1
-        while bit < lax.axis_size(axis):
-            bits.append((axis, bit))
-            bit *= 2
-    return bits
+def axis_sizes():
+    return [(axis, lax.axis_size(axis)) for axis in ("samp", "seq")]
 
 
 def sum_kernel(parts, streams, *refs):
@@ -389,19 +383,22 @@
 
     gtok_ref, rsum_ref = grads[1], grads[3]
     width = grads[0].shape[0]
-    bits = axis_bits()
-    count = len(bits)
-    sends, recvs = slots[: streams * count], slots[streams * count :]
-    where = []
-    for axis, bit in bits:
-        me = lax.axis_index(axis)
-        upper = lax.rem(me // bit, 2)
-        where.append((upper, {axis: me + bit - 2 * bit * upper}))
+    axes = axis_sizes()
+    peers = sum(size - 1 for _, size in axes)
+    sends, recvs = slots[: 2 * streams], slots[2 * streams :]
+
+    def peer(axis, size, distance):
+        return lax.rem(lax.axis_index(axis) + distance, size)
+
     barrier = pltpu.get_barrier_semaphore()
-    for _, partner in where:
-        pl.semaphore_signal(
-            barrier, inc=1, device_id=partner, device_id_type=pl.DeviceIdType.MESH
-        )
+    for axis, size in axes:
+        for d in range(1, size):
+            pl.semaphore_signal(
+                barrier,
+                inc=1,
+                device_id={axis: peer(axis, size, d)},
+                device_id_type=pl.DeviceIdType.MESH,
+            )
 
     every = slice(None)
     blocks = gtok_ref.shape[1] // width
@@ -427,65 +424,73 @@
             ]
     spot = at + HEADS * (wide // width)
     buf[spot : spot + 1, :] = total(4)
-    pl.semaphore_wait(barrier, count)
-
-    size = buf.shape[0] // streams
-    orders = []
-    for stream in range(streams):
-        order = list(range(count))
-        turn = (stream * 2) % 3
-        order[:3] = order[turn:3] + order[:turn]
-        orders.append(order)
-    offs = [stream * size for stream in range(streams)]
-    lengths = [size] * streams
-    pending = [None] * streams
+    pl.semaphore_wait(barrier, peers)
+
+    unit = buf.shape[0] // streams
+    orders = [axes[::-1] if stream % 3 == 1 else axes for stream in range(streams)]
+    offs = [stream * unit for stream in range(streams)]
+    lengths = [unit] * streams
+    pending = [[] for _ in range(streams)]
 
     def send(stream, src, dst, slot, partner):
         copy = pltpu.make_async_remote_copy(
             src_ref=src,
             dst_ref=dst,
-            send_sem=send_sem.at[stream * 2 * count + slot],
-            recv_sem=recv_sem.at[stream * 2 * count + slot],
+            send_sem=send_sem.at[stream * 2 * peers + slot],
+            recv_sem=recv_sem.at[stream * 2 * peers + slot],
             device_id=partner,
             device_id_type=pl.DeviceIdType.MESH,
         )
         copy.start()
-        pending[stream] = copy
+        pending[stream].append(copy)
 
     def absorb(stream, k):
-        pending[stream].wait()
-        rows = pl.ds(offs[stream], lengths[stream])
-        buf[rows, :] = buf[rows, :] + recvs[stream * count + k][...].astype(F32)
-
-    for k in range(count):
+        rows = pl.ds(pl.multiple_of(offs[stream], 16), lengths[stream])
+        value = buf[rows, :]
+        for n, copy in enumerate(pending[stream]):
+            copy.wait()
+            value = value + recvs[2 * stream + k][n].astype(F32)
+        pending[stream] = []
+        return rows, value
+
+    for k in range(2):
         for stream in range(streams):
+            axis, size = orders[stream][k]
+            base = 0
             if k > 0:
-                absorb(stream, k - 1)
-            upper, partner = where[orders[stream][k]]
-            lengths[stream] //= 2
+                rows, value = absorb(stream, k - 1)
+                buf[rows, :] = value
+                base = orders[stream][0][1] - 1
+            length = lengths[stream] // size
+            for d in range(1, size):
+                to = peer(axis, size, d)
+                give = pl.multiple_of(offs[stream] + to * length, 16)
+                slot = sends[2 * stream + k].at[d - 1]
+                slot[...] = buf[pl.ds(give, length), :].astype(BF16)
+                send(stream, slot, recvs[2 * stream + k].at[d - 1], base + d - 1, {axis: to})
+            lengths[stream] = length
+            offs[stream] = offs[stream] + lax.axis_index(axis) * length
+    for k in (1, 0):
+        for stream in range(streams):
+            axis, size = orders[stream][k]
+            base = peers
+            if k == 1:
+                rows, value = absorb(stream, 1)
+                out_ref[rows, :] = value.astype(BF16)
+            else:
+                for copy in pending[stream]:
+                    copy.wait()
+                pending[stream] = []
+                base += orders[stream][1][1] - 1
             length = lengths[stream]
-            keep = pl.multiple_of(offs[stream] + upper * length, 16)
-            give = pl.multiple_of(offs[stream] + (1 - upper) * length, 16)
-            slot = sends[stream * count + k]
-            slot[...] = buf[pl.ds(give, length), :].astype(BF16)
-            send(stream, slot, recvs[stream * count + k], k, partner)
-            offs[stream] = keep
-    for k in range(count - 1, -1, -1):
-        for stream in range(streams):
-            upper, partner = where[orders[stream][k]]
-            length = lengths[stream]
-            if k == count - 1:
-                absorb(stream, k)
-                rows = pl.ds(offs[stream], length)
-                out_ref[rows, :] = buf[rows, :].astype(BF16)
-            else:
-                pending[stream].wait()
             part = out_ref.at[pl.ds(pl.multiple_of(offs[stream], 16), length), :]
-            send(stream, part, part, count + k, partner)
-            offs[stream] = offs[stream] - upper * length
-            lengths[stream] *= 2
+            for d in range(1, size):
+                send(stream, part, part, base + d - 1, {axis: peer(axis, size, d)})
+            offs[stream] = offs[stream] - lax.axis_index(axis) * length
+            lengths[stream] = length * size
     for stream in range(streams):
-        pending[stream].wait()
+        for copy in pending[stream]:
+            copy.wait()
 
 
 def unpack_kernel(packed_ref, gq_out, gk_out, gv_out, gg_out, gout_out, gtok_out, small_out):
@@ -507,12 +512,19 @@
     shape = jax.ShapeDtypeStruct
     gout, gtok, gw = halves[0][:3]
     width = gout.shape[0]
-    count = len(axis_bits())
-    unit = 16 * 2**count
+    axes = axis_sizes()
+    devices = axes[0][1] * axes[1][1]
+    peers = sum(size - 1 for _, size in axes)
+    unit = 16 * devices
     lines = gtok.shape[1] + gw.shape[1] + width + 16
     total = -(-lines // unit) * unit
     streams = total // unit
-    slots = [pltpu.VMEM((unit >> (k + 1), width), BF16) for k in range(count)]
+    slots = []
+    for stream in range(streams):
+        length = unit
+        for _, size in axes[::-1] if stream % 3 == 1 else axes:
+            length //= size
+            slots.append(pltpu.VMEM((size - 1, length, width), BF16))
     operands = [x for half in halves for x in half]
     vmem = pl.BlockSpec(memory_space=pltpu.VMEM)
     packed = pl.pallas_call(
@@ -522,10 +534,10 @@
         out_shape=shape((total, width), BF16),
         scratch_shapes=[
             pltpu.VMEM((total, width), F32),
-            pltpu.SemaphoreType.DMA((2 * streams * count,)),
-            pltpu.SemaphoreType.DMA((2 * streams * count,)),
+            pltpu.SemaphoreType.DMA((2 * streams * peers,)),
+            pltpu.SemaphoreType.DMA((2 * streams * peers,)),
         ]
-        + slots * (2 * streams),
+        + slots * 2,
         compiler_params=pltpu.CompilerParams(collective_id=0, has_side_effects=True),
     )(*operands)
     return pl.pallas_call(
@@ -596,8 +608,8 @@
         specs = [
             pl.BlockSpec(memory_space=pltpu.SMEM),
             per_sample(rows, width, base=base),
-            per_sample(rim, width),
-            per_sample(rim, width),
+            per_sample(rim, width, base=base),
+            per_sample(rim, width, base=base),
             whole(1, width),
             square,
             square,
@@ -738,14 +750,11 @@
 
     first = samples // 2
     cuts = [(0, first), (first, samples - first)]
-    rims = []
-    for base, count in cuts:
-        low = shifted(atoms[base : base + count, rows - rim :], "seq", 1)
-        high = shifted(atoms[base : base + count, :rim], "seq", -1)
-        rims.append((low, high))
+    low = shifted(atoms[:, rows - rim :], "seq", 1)
+    high = shifted(atoms[:, :rim], "seq", -1)
     pooled = None
     mains = []
-    for (base, count), (low, high) in zip(cuts, rims):
+    for base, count in cuts:
         outs = run_main(base, count, low, high, pooled)
         pooled = outs[0]
         _, gupd, dq, dkv, edge_low, edge_high, dg, gout, gtok, rsum = outs

time: 155 us -> 141 us (0.910)
  Pallas kernels: 120 us -> 111 us
  starting transfers between devices: 25.7 us -> 18.5 us
  waiting for transfers between devices: 0.02 us -> 3.56 us
    pallas_call x1, Pallas kernels: 34.5 us -> 25.3 us  [sum_all(): pl.pallas_call(functools.partial(sum_kernel, len(halves), streams), in_sp...]
    ppermute x8 -> x6, starting transfers between devices: 25.7 us -> 18.5 us  [shifted(): return lax.ppermute(block, axis, route)]
    ppermute x8 -> x6, waiting for transfers between devices: 0.02 us -> 3.56 us  [shifted(): return lax.ppermute(block, axis, route)]
  transfers between devices with their start and end apart: 8 -> 6, of which waited for: 0 -> 2; matrix products, arithmetic and copies ran while one was open for 1% -> 1% of each run, Pallas kernels for 49% -> 30%
where the time goes in v4:
time: 141 us
  Pallas kernels  111 us (79%)
  starting transfers between devices  18.5 us (13%)
  local copies, waits for them, and re-layouts  5.87 us (4%)
  waiting for transfers between devices  3.56 us (3%)
    pallas_call x2, Pallas kernels, run_main(): pl.pallas_call(main_kernel if before is None else dropping(main_kernel, p...  68.8 us
    pallas_call x1, Pallas kernels, sum_all(): pl.pallas_call(functools.partial(sum_kernel, len(halves), streams), in_sp...  25.3 us
    ppermute x6, starting transfers between devices, shifted(): return lax.ppermute(block, axis, route)  18.5 us
    pallas_call x2, Pallas kernels, run_tail(): pl.pallas_call(tail_kernel if before is None else dropping(tail_kernel, p...  14.6 us
    ppermute x6, waiting for transfers between devices, shifted(): return lax.ppermute(block, axis, route)  3.56 us
  transfers between devices with their start and end apart: 6, of which 2 were waited for; matrix products, arithmetic and copies ran while one was open for 1% of the time, Pallas kernels for 30%

profile of v4, /device:TPU:0, one launch (start us, length us, event | category | flops | bytes accessed | tf_op | source)
XLA Modules:
  0.0 140.7 jit_solution(18408346198721249532)
XLA Ops:
  0.6 1.0 fusion.1
  1.7 1.3 collective-permute-start.1
  3.0 5.5 %collective-permute-start = (bf16[12,48,128]{2,1,0:T(8,128)(2,1)S(1)}, bf16[12,48,128]{2,1,0:T(8,128)(2,1)S(1)}, u32[]{:S(2)}, u32[]{:S(2)}) collective-permute-start(bf16[12,48,128]{2,1,0:T(8,128)(2,1)S(1)} %get-tuple-element.77), channel_id=1, source_target_pairs={{0,4},{4,8},{8,12},{12,16},{16,20},{20,24},{24,28},{1,5},{5,9},{9,... | collective-permute-start | bytes 442376 | tf_op jit(solution)/shard_map/ppermute | solution.py:570
  8.5 0.8 broadcast_multiply_fusion
  9.3 0.9 mul.20.wsm_ref.refs_11_
  10.2 0.2 collective-permute-done.1.high_ref.refs_3_
  10.4 3.3 %collective-permute-done.low_ref.refs_2_ = bf16[12,48,128]{2,1,0:T(8,128)(2,1)S(1)} collective-permute-done((bf16[12,48,128]{2,1,0:T(8,128)(2,1)S(1)}, bf16[12,48,128]{2,1,0:T(8,128)(2,1)S(1)}, u32[]{:S(2)}, u32[]{:S(2)}) %collective-permute-start) | collective-permute-done | bytes 147488 | tf_op jit(solution)/shard_map/ppermute | solution.py:570
  13.7 0.7 copy-done.1
  14.4 34.3 %shard_map.204 = (bf16[12,48,768]{2,1,0:T(8,128)(2,1)}, bf16[6,512,128]{2,1,0:T(8,128)(2,1)}, bf16[6,512,128]{2,1,0:T(8,128)(2,1)}, bf16[6,512,256]{2,1,0:T(8,12...) custom-call(s32[8]{0:T(128)} %refs_0_.2, ...), custom_call_target="tpu_custom_call" | custom-call | flops 12288000000 | bytes 4194304 | tf_op jit(solution)/shard_map/pallas_call | solution.py:643
  48.7 4.4 %collective-permute-start.4 = (bf16[6,48,256]{2,1,0:T(8,128)(2,1)}, bf16[6,48,256]{2,1,0:T(8,128)(2,1)S(1)}, u32[]{:S(2)}, u32[]{:S(2)}) collective-permute-start(bf16[6,48,256]{2,1,0:T(8,128)(2,1)} %get-tuple-element.54), channel_id=1, source_target_pairs={{0,4},{4,8},{8,12},{12,16},{16,20},{20,24},{24,28},{1,5},{5,9},{9,... | collective-permute-start | bytes 442376 | tf_op jit(solution)/shard_map/ppermute | solution.py:570
  53.1 1.5 %collective-permute-start.5 = (bf16[6,48,256]{2,1,0:T(8,128)(2,1)}, bf16[6,48,256]{2,1,0:T(8,128)(2,1)S(1)}, u32[]{:S(2)}, u32[]{:S(2)}) collective-permute-start(bf16[6,48,256]{2,1,0:T(8,128)(2,1)} %get-tuple-element.55), channel_id=1, source_target_pairs={{4,0},{8,4},{12,8},{16,12},{20,16},{24,20},{28,24},{5,1},{9,5},{13... | collective-permute-start | bytes 442376 | tf_op jit(solution)/shard_map/ppermute | solution.py:570
  54.6 34.4 %shard_map.205 = (bf16[12,48,768]{2,1,0:T(8,128)(2,1)}, bf16[6,512,128]{2,1,0:T(8,128)(2,1)}, bf16[6,512,128]{2,1,0:T(8,128)(2,1)}, bf16[6,512,256]{2,1,0:T(8,12...) custom-call(s32[8]{0:T(128)} %refs_0_.2, ...), custom_call_target="tpu_custom_call", output_to_operand_aliasing={{0}: (15, {})} | custom-call | flops 12288000000 | bytes 4194304 | tf_op jit(solution)/shard_map/pallas_call | solution.py:643
  89.0 4.6 %collective-permute-start.2 = (bf16[6,48,256]{2,1,0:T(8,128)(2,1)}, bf16[6,48,256]{2,1,0:T(8,128)(2,1)S(1)}, u32[]{:S(2)}, u32[]{:S(2)}) collective-permute-start(bf16[6,48,256]{2,1,0:T(8,128)(2,1)} %get-tuple-element.48), channel_id=1, source_target_pairs={{0,4},{4,8},{8,12},{12,16},{16,20},{20,24},{24,28},{1,5},{5,9},{9,... | collective-permute-start | bytes 442376 | tf_op jit(solution)/shard_map/ppermute | solution.py:570
  93.6 1.3 collective-permute-start.3
  94.9 0.6 copy-done.2
  95.6 0.1 copy-done.3
  95.7 7.3 %shard_map.206 = (bf16[12,512,128]{2,1,0:T(8,128)(2,1)}, f32[1,128]{1,0:T(1,128)}, f32[128,512]{1,0:T(8,128)}) custom-call(bf16[12,512,128]{2,1,0:T(8,128)(2,1)} %refs_0_.3, f32[1,128]{1,0:T(1,128)} %bitcast.17, bf16[128,128]{1,0:T(8,128)(2,1)} %refs_2_.1, bf16[128,128]{1,0:T(8,128)(2,1)} %refs_3_.1, bf16[128,128]{1,0:T(8,128)(2,1)} %refs_4_.1, ...), custom_call_target="tpu_custom_call" | custom-call | flops 2457600000 | bytes 4194304 | tf_op jit(solution)/shard_map/pallas_call | solution.py:712
  103.0 0.6 copy-done.4
  103.7 7.3 %shard_map.207 = (bf16[12,512,128]{2,1,0:T(8,128)(2,1)}, f32[1,128]{1,0:T(1,128)}, f32[128,512]{1,0:T(8,128)}) custom-call(bf16[12,512,128]{2,1,0:T(8,128)(2,1)} %refs_0_.3, f32[1,128]{1,0:T(1,128)} %bitcast.18, bf16[128,128]{1,0:T(8,128)(2,1)} %refs_2_.1, bf16[128,128]{1,0:T(8,128)(2,1)} %refs_3_.1, ...), custom_call_target="tpu_custom_call", output_to_operand_aliasing={{0}: (12, {})} | custom-call | flops 2457600000 | bytes 4194304 | tf_op jit(solution)/shard_map/pallas_call | solution.py:712
  111.0 25.3 %shard_map.208.packed_ref = bf16[1536,128]{1,0:T(8,128)(2,1)} custom-call(f32[128,128]{1,0:T(8,128)} %get-tuple-element.59.refs_0_, f32[128,768]{1,0:T(8,128)} %get-tuple-element.60.refs_1_, f32[128,512]{1,0:T(8,128)} %get-tuple-element.61.refs_2_, f32[64,256]{1,0:T(8,128)} %get-tuple-element.62.refs_3_, f32[1,128]{1,0:T(1,128)} %get-tuple-element.63.refs_4_, ...), custom_call_target="tpu_custom_call" | custom-call | tf_op jit(solution)/shard_map/pallas_call | solution.py:530
  136.3 1.9 %shard_map.209 = (f32[128,128]{1,0:T(8,128)}, f32[128,128]{1,0:T(8,128)}, f32[128,128]{1,0:T(8,128)}, f32[128,128]{1,0:T(8,128)}, f32[128,128]{1,0:T(8,128)}, /*index=5*/f32[128,768]{1,0:T(8,128)}, f32[16,128]{1,0:T(8,128)}) custom-call(bf16[1536,128]{1,0:T(8,128)(2,1)} %shard_map.208.packed_ref), custom_call_target="tpu_custom_call" | custom-call | tf_op jit(solution)/shard_map/pallas_call | solution.py:543
  138.2 1.2 slice_bitcast_fusion
  139.4 0.7 slice.15
  140.1 0.6 reduce_sum.9
  (14 shorter events, 0.2 us)
Async XLA Ops:
  1.7 8.7 %collective-permute-start.1 = (bf16[12,48,128]{2,1,0:T(8,128)(2,1)S(1)}, bf16[12,48,128]{2,1,0:T(8,128)(2,1)S(1)}, u32[]{:S(2)}, u32[]{:S(2)}) collective-permute-start(bf16[12,48,128]{2,1,0:T(8,128)(2,1)S(1)} %get-tuple-element.76), channel_id=1, source_target_pairs={{4,0},{8,4},{12,8},{16,12},{20,16},{24,20},{28,24},{5,1},{9,5},{13... | collective-permute-start | bytes 442376 | tf_op jit(solution)/shard_map/ppermute | solution.py:570
  3.0 10.8 %collective-permute-start = (bf16[12,48,128]{2,1,0:T(8,128)(2,1)S(1)}, bf16[12,48,128]{2,1,0:T(8,128)(2,1)S(1)}, u32[]{:S(2)}, u32[]{:S(2)}) collective-permute-start(bf16[12,48,128]{2,1,0:T(8,128)(2,1)S(1)} %get-tuple-element.77), channel_id=1, source_target_pairs={{0,4},{4,8},{8,12},{12,16},{16,20},{20,24},{24,28},{1,5},{5,9},{9,... | collective-permute-start | bytes 442376 | tf_op jit(solution)/shard_map/ppermute | solution.py:570
  10.4 3.3 %copy-start = (bf16[12,48,128]{2,1,0:T(8,128)(2,1)}, bf16[12,48,128]{2,1,0:T(8,128)(2,1)S(1)}, u32[]{:S(2)}) copy-start(bf16[12,48,128]{2,1,0:T(8,128)(2,1)S(1)} %collective-permute-done.1.high_ref.refs_3_) | copy-start | bytes 442372
  13.7 0.7 copy-start.1
  48.7 46.2 %collective-permute-start.4 = (bf16[6,48,256]{2,1,0:T(8,128)(2,1)}, bf16[6,48,256]{2,1,0:T(8,128)(2,1)S(1)}, u32[]{:S(2)}, u32[]{:S(2)}) collective-permute-start(bf16[6,48,256]{2,1,0:T(8,128)(2,1)} %get-tuple-element.54), channel_id=1, source_target_pairs={{0,4},{4,8},{8,12},{12,16},{16,20},{20,24},{24,28},{1,5},{5,9},{9,... | collective-permute-start | bytes 442376 | tf_op jit(solution)/shard_map/ppermute | solution.py:570
  53.1 41.8 %collective-permute-start.5 = (bf16[6,48,256]{2,1,0:T(8,128)(2,1)}, bf16[6,48,256]{2,1,0:T(8,128)(2,1)S(1)}, u32[]{:S(2)}, u32[]{:S(2)}) collective-permute-start(bf16[6,48,256]{2,1,0:T(8,128)(2,1)} %get-tuple-element.55), channel_id=1, source_target_pairs={{4,0},{8,4},{12,8},{16,12},{20,16},{24,20},{28,24},{5,1},{9,5},{13... | collective-permute-start | bytes 442376 | tf_op jit(solution)/shard_map/ppermute | solution.py:570
  89.0 13.9 %collective-permute-start.2 = (bf16[6,48,256]{2,1,0:T(8,128)(2,1)}, bf16[6,48,256]{2,1,0:T(8,128)(2,1)S(1)}, u32[]{:S(2)}, u32[]{:S(2)}) collective-permute-start(bf16[6,48,256]{2,1,0:T(8,128)(2,1)} %get-tuple-element.48), channel_id=1, source_target_pairs={{0,4},{4,8},{8,12},{12,16},{16,20},{20,24},{24,28},{1,5},{5,9},{9,... | collective-permute-start | bytes 442376 | tf_op jit(solution)/shard_map/ppermute | solution.py:570
  93.6 9.4 %collective-permute-start.3 = (bf16[6,48,256]{2,1,0:T(8,128)(2,1)}, bf16[6,48,256]{2,1,0:T(8,128)(2,1)S(1)}, u32[]{:S(2)}, u32[]{:S(2)}) collective-permute-start(bf16[6,48,256]{2,1,0:T(8,128)(2,1)} %get-tuple-element.49), channel_id=1, source_target_pairs={{4,0},{8,4},{12,8},{16,12},{20,16},{24,20},{28,24},{5,1},{9,5},{13... | collective-permute-start | bytes 442376 | tf_op jit(solution)/shard_map/ppermute | solution.py:570
  94.9 0.7 copy-start.2
  94.9 0.7 copy-start.3
  102.9 0.7 copy-start.4
  103.0 0.7 copy-start.5
